TPU v7x, 128 devices: a whole 4x4x4 slice. The times are simulated.
128 devices in a mesh: tile: 32 (over y, z, core), row: 4 (over x).
Axes of the slice: x: 4, y: 4, z: 4, core: 2. Of those that a mesh axis runs over, the one named last changes fastest.
Arguments:
- cam_disp: bfloat16 [4, 32, 4, 2, 256, 512], P('row', 'tile')
- footprint: int32 [4, 32, 2, 2], P('row', 'tile'), may hold values from 0 to 15, as said below
- stencil: int32 [4, 32, 2, 2, 2, 256], P('row', 'tile'), may hold values from 0 to 12
- frac: float32 [4, 32, 2, 2, 2, 256], P('row', 'tile'), may hold values from 0 to 1
- coef: float32 [4, 32, 2, 3, 4, 256], P('row', 'tile'), may hold values from -3 to 3
Outputs:
- velocity: bfloat16 [4, 32, 2, 3, 256, 512], P('row', 'tile')
- rfactor: float32 [512, 512], replicated
Inputs may be any that keep to these rules, and one draw needn't show every extreme that they name: `footprint`: for each device, the camera tiles named for camera 0 all lie in one row group and are distinct; those for camera 1 lie in other row groups. So a device needs at most 2 distinct camera tiles from any one row group, and exactly 2 from one of them.
All inputs are finite; a program needn't handle non-finite values.
Results may differ from a plain program's by a relative error of at most 0.0015.
The roundings to bfloat16 on the way count: a program that leaves them out, or rounds other values in their place, can miss the bound.
Values may be sent and summed in bfloat16 or wider, within the bound.
No kernel may reach another device: no remote copies, remote signals or barrier semaphores. Data moves between devices by JAX's collectives and lax.ppermute only.
A program may use at most 512 MiB of HBM per device.

v0:
```python
import functools

import jax
import jax.numpy as jnp
from jax import lax
from jax.experimental import pallas as pl
from jax.experimental.pallas import tpu as pltpu
from jax.sharding import Mesh, PartitionSpec as P


F32 = jnp.float32
BF16 = jnp.bfloat16
TILE_SIDE = 16
EARLY = 32
HALVES = (((0, 3), (1, 3), (2, 3), (3, 3), (0, 0)), ((0, 2), (1, 2), (2, 2), (0, 1), (1, 1)))
PLACE = {block: (half, at) for half, blocks in enumerate(HALVES) for at, block in enumerate(blocks)}
PLANE = ("y", "z")
ANY = pl.BlockSpec(memory_space=pl.ANY)
VM = pl.BlockSpec(memory_space=pltpu.VMEM)


def catmull(t):
    k0 = ((-0.5 * t + 1.0) * t - 0.5) * t
    k1 = (1.5 * t - 2.5) * t * t + 1.0
    k2 = ((-1.5 * t + 2.0) * t + 0.5) * t
    k3 = (0.5 * t - 0.5) * t * t
    return (k0, k1, k2, k3)


def prepare_kernel(sten_ref, frac_ref, coef_ref, mats_ref, columns_ref):
    pairs, cells = sten_ref.shape[0], sten_ref.shape[2]
    pix = mats_ref.shape[3]
    rows = []
    for p in range(pairs):
        for axis in range(2):
            rows.append(sten_ref[p, axis : axis + 1, :].astype(F32))
            rows.extend(catmull(frac_ref[p, axis : axis + 1, :]))
    for w in range(coef_ref.shape[0]):
        rows.append(coef_ref[w])
    used = sum(r.shape[0] for r in rows)
    rows.append(jnp.zeros((128 - used, cells), F32))
    table = jnp.concatenate(rows, axis=0).T
    columns_ref[...] = table
    lane = lax.broadcasted_iota(jnp.int32, (cells, pix), 1)
    spots = ((lane // TILE_SIDE).astype(F32), (lane % TILE_SIDE).astype(F32))
    for p in range(pairs):
        product = None
        for axis in range(2):
            at = 10 * p + 5 * axis
            offset = spots[axis] - table[:, at : at + 1]
            weight = jnp.zeros((cells, pix), F32)
            for shift in range(4):
                weight = jnp.where(offset == float(shift), table[:, at + 1 + shift : at + 2 + shift], weight)
            product = weight if product is None else product * weight
        mats_ref[p // 2, p % 2] = product.astype(BF16)


def prepare(sten, frac, coef, pix):
    pairs, _, cells = sten.shape
    return pl.pallas_call(
        prepare_kernel,
        out_shape=(
            jax.ShapeDtypeStruct((pairs // 2, 2, cells, pix), BF16),
            jax.ShapeDtypeStruct((cells, 128), F32),
        ),
        in_specs=[VM] * 3,
        out_specs=(VM, VM),
        compiler_params=pltpu.CompilerParams(vmem_limit_bytes=8 << 20),
        cost_estimate=pl.CostEstimate(flops=4_000_000, bytes_accessed=1_000_000, transcendentals=0),
        name="prepare",
    )(sten, frac, coef)


def early_kernel(ids_ref, cam_ref, ids_out, out, sem):
    copies = [pltpu.make_async_copy(cam_ref.at[t, :, pl.ds(0, EARLY)], out.at[t], sem.at[t]) for t in range(cam_ref.shape[0])]
    for copy in copies:
        copy.start()
    ids_out[...] = ids_ref[...]
    for copy in copies:
        copy.wait()


def early(ids, tiles):
    count, parts, _, snaps = tiles.shape
    return pl.pallas_call(
        early_kernel,
        out_shape=[jax.ShapeDtypeStruct(ids.shape, ids.dtype), jax.ShapeDtypeStruct((count, parts, EARLY, snaps), tiles.dtype)],
        in_specs=[VM, ANY],
        out_specs=[VM, VM],
        scratch_shapes=[pltpu.SemaphoreType.DMA((count,))],
        compiler_params=pltpu.CompilerParams(vmem_limit_bytes=4 << 20),
        cost_estimate=pl.CostEstimate(flops=0, bytes_accessed=500_000, transcendentals=0),
        name="early",
    )(ids, tiles)


def select_kernel(ids_ref, cam_ref, *rest):
    outs, sem = rest[:-1], rest[-1]
    me = lax.axis_index("x")
    count, _, pix, _ = cam_ref.shape
    copies = []
    for w, out in enumerate(outs):
        first, second = ids_ref[w, 0], ids_ref[w, 1]
        own = lax.shift_right_logical(first, 2) == me
        index = jnp.where(own, first, second) & (count - 1)
        copies.append(pltpu.make_async_copy(cam_ref.at[index, :, pl.ds(EARLY, pix - EARLY)], out, sem.at[w]))
        copies[-1].start()
    for copy in copies:
        copy.wait()


def select(ids, tiles):
    world_tiles = ids.shape[0]
    _, parts, pix, snaps = tiles.shape
    return pl.pallas_call(
        select_kernel,
        out_shape=[jax.ShapeDtypeStruct((parts, pix - EARLY, snaps), tiles.dtype)] * world_tiles,
        in_specs=[pl.BlockSpec(memory_space=pltpu.SMEM), ANY],
        out_specs=[VM] * world_tiles,
        scratch_shapes=[pltpu.SemaphoreType.DMA((world_tiles,))],
        compiler_params=pltpu.CompilerParams(vmem_limit_bytes=4 << 20),
        cost_estimate=pl.CostEstimate(flops=0, bytes_accessed=2_000_000, transcendentals=0),
    )(ids, tiles)


def world_kernel(w, ids_ref, cam_ref, e1_ref, e2_ref, e3_ref, r1_ref, r2_ref, r3_ref, mats_ref, coef_ref, *rest):
    if w:
        gin_ref, _, vel_ref, mine_ref, other_ref, tiles, interp, sem = rest
    else:
        vel_ref, gram_ref, tiles, interp, sem = rest
    cells, snaps = vel_ref.shape[2], vel_ref.shape[3]
    firsts, others = (None, e1_ref, e2_ref, e3_ref), (None, r1_ref, r2_ref, r3_ref)
    indices, dists = [], []
    for c in range(2):
        tile = ids_ref[w, c]
        index, dist = tile & 3, lax.shift_right_logical(tile, 2) ^ lax.axis_index("x")
        indices.append(index)
        dists.append(dist)

        @pl.when(dist == 0)
        def _():
            pltpu.make_async_copy(cam_ref.at[index], tiles.at[c], sem.at[c]).start()

    for c in range(2):
        for k in range(4):

            @pl.when(dists[c] == k)
            def _():
                if k == 0:
                    pltpu.make_async_copy(cam_ref.at[0], tiles.at[c], sem.at[c]).wait()
                else:
                    tiles[c, :, :EARLY] = firsts[k][indices[c]]
                    tiles[c, :, EARLY:] = others[k][...]

        for j in range(2):
            interp[2 * c + j] = jnp.dot(mats_ref[w, c], tiles[c, j], preferred_element_type=F32)

    rows = 32

    def cell_rows(step, _):
        q = pl.ds(pl.multiple_of(step * rows, rows), rows)
        parts = [interp[i, q, :] for i in range(4)]
        for k in range(3):
            at = 40 + 12 * w + 4 * k
            total = coef_ref[q, at : at + 1] * parts[0]
            for i in range(1, 4):
                total = total + coef_ref[q, at + i : at + i + 1] * parts[i]
            vel_ref[0, k, q, :] = total.astype(BF16)
        return 0

    lax.fori_loop(0, cells // rows, cell_rows, 0)
    flat = vel_ref[0].reshape(3 * cells, snaps)
    core = lax.axis_index("core")
    for i in range(snaps // 256):
        left = flat[:, 256 * i : 256 * (i + 1)]
        block = lax.dot_general(left, flat[:, 256 * i :], (((0,), (0,)), ((), ())), preferred_element_type=F32)
        parts = []
        for row in (2 * i, 2 * i + 1):
            for column in range(row, snaps // 128):
                half, at = PLACE[row, column]
                part = block[128 * row - 256 * i : 128 * (row + 1) - 256 * i, 128 * column - 256 * i : 128 * (column + 1) - 256 * i]
                if w == 0:
                    gram_ref[half, at] = part
                else:
                    parts.append((half, at, part + gin_ref[half, at]))
        if w == 0:
            continue
        for side in range(2):

            @pl.when(core == side)
            def _():
                for half, at, part in parts:
                    (mine_ref if half == side else other_ref)[at] = part


def world(w, ids, cam, firsts, recv, mats, coef, carry):
    snaps, cells = cam.shape[-1], mats.shape[2]
    world_tiles = 2
    outs = 2 if w else 1
    grams = (len(HALVES[0]), 128, 128) if w else (2, len(HALVES[0]), 128, 128)
    in_specs = [pl.BlockSpec(memory_space=pltpu.SMEM), ANY] + [VM] * 8
    args = [ids, cam, *firsts, *recv, mats, coef]
    aliases = {}
    if w:
        in_specs += [VM, ANY]
        args += [carry[1], carry[0]]
        aliases = {len(args) - 1: 0}
    return pl.pallas_call(
        functools.partial(world_kernel, w),
        grid=(1,),
        in_specs=in_specs,
        out_specs=(
            pl.BlockSpec((1, 3, cells, snaps), lambda _: (w, 0, 0, 0)),
            *[pl.BlockSpec(grams, lambda _: (0,) * len(grams))] * outs,
        ),
        out_shape=(
            jax.ShapeDtypeStruct((world_tiles, 3, cells, snaps), BF16),
            *[jax.ShapeDtypeStruct(grams, F32)] * outs,
        ),
        scratch_shapes=[
            pltpu.VMEM((2, 2, cam.shape[2], snaps), BF16),
            pltpu.VMEM((4, cells, snaps), F32),
            pltpu.SemaphoreType.DMA((2,)),
        ],
        input_output_aliases=aliases,
        compiler_params=pltpu.CompilerParams(vmem_limit_bytes=16 << 20),
        cost_estimate=pl.CostEstimate(flops=700_000_000, bytes_accessed=4_000_000, transcendentals=0),
    )(*args)


def spread(x, k):
    return jnp.broadcast_to(x[k % 8 : k % 8 + 1, :], x.shape)


def inverse_factor(blocks, size=16):
    width, per = blocks[0].shape[1], size // 8
    lane = lax.broadcasted_iota(jnp.int32, (8, width), 1)
    sub = lax.broadcasted_iota(jnp.int32, (8, width), 0)
    is_row = [sub == k for k in range(8)]
    slabs, out = list(blocks), []
    for s in range(len(blocks) // per):
        k0 = size * s
        own = slabs[s * per : (s + 1) * per]
        columns = [[jnp.broadcast_to(a[:, k0 + j : k0 + j + 1], (8, width)) for a in own] for j in range(size)]
        inside = (lane >= k0) & (lane < k0 + size)
        rows = [jnp.where(inside, jnp.where(lane - k0 - 8 * v == sub, 1.0, 0.0), a) for v, a in enumerate(own)]
        scaled = [None] * per
        for k in range(size):
            at, here = k // 8, is_row[k % 8]
            root = lax.rsqrt(spread(columns[k][at], k))
            inverse = root * root
            row = spread(rows[at], k)
            final = row * root
            scaled[at] = final if scaled[at] is None else jnp.where(here, final, scaled[at])
            t = row * inverse
            for j in range(k + 1, size):
                ct = spread(columns[j][at], k) * inverse
                new = [columns[j][v] - columns[k][v] * ct for v in range(per)]
                new[at] = jnp.where(here, ct, new[at])
                columns[j] = new
            new = [rows[v] - columns[k][v] * t for v in range(per)]
            new[at] = jnp.where(here, t, new[at])
            rows = new
        out.extend(jnp.where(lane < k0 + size, x, 0.0) for x in scaled)
        solved = [spread(rows[k // 8], k) for k in range(size)]
        for b in range((s + 1) * per, len(blocks)):
            x = slabs[b]
            totals = [jnp.where(inside, 0.0, x), 0.0]
            for k in range(size):
                totals[k % 2] = totals[k % 2] - jnp.broadcast_to(x[:, k0 + k : k0 + k + 1], (8, width)) * solved[k]
            slabs[b] = totals[0] + totals[1]
    return out


def exact_dot(a, b, dims):
    return lax.dot_general(a, b, ((dims[:1], dims[1:]), ((), ())), precision=lax.Precision.HIGHEST, preferred_element_type=F32)


def factor_kernel(own_ref, other_ref, o_ref, s_ref):
    n, size = o_ref.shape[0], 128
    parts = n // size
    core = lax.axis_index("core")
    for side in range(2):

        @pl.when(core == side)
        def _():
            for half, ref in ((side, own_ref), (1 - side, other_ref)):
                for at, (row, column) in enumerate(HALVES[half]):
                    s_ref[row * size : (row + 1) * size, column * size : (column + 1) * size] = ref[at]

    o_ref[...] = jnp.zeros_like(o_ref)

    def panel(p, _):
        off = pl.multiple_of(p * size, size)
        blocks = [s_ref[pl.ds(off + 8 * i, 8), pl.ds(off, size)] for i in range(size // 8)]
        linv = jnp.concatenate(inverse_factor(blocks), axis=0)
        for q in range(parts):

            @pl.when(p == q)
            def _():
                lo, wide = q * size, n - q * size
                r = exact_dot(linv, s_ref[lo : lo + size, lo:], (1, 0))
                row = lax.broadcasted_iota(jnp.int32, (size, wide), 0)
                col = lax.broadcasted_iota(jnp.int32, (size, wide), 1)
                r = jnp.where(col >= row, r, 0.0)
                o_ref[lo : lo + size, lo:] = r
                if q < parts - 1:
                    for m in range(q + 1, parts):
                        at = m * size
                        t = r[:, at - lo :]
                        s_ref[at : at + size, at:] = s_ref[at : at + size, at:] - exact_dot(t[:, :size], t, (0, 0))

        return 0

    lax.fori_loop(0, parts, panel, 0)


def factor(own, other, n):
    return pl.pallas_call(
        factor_kernel,
        out_shape=jax.ShapeDtypeStruct((n, n), F32),
        in_specs=[VM, VM],
        out_specs=VM,
        scratch_shapes=[pltpu.VMEM((n, n), F32)],
        compiler_params=pltpu.CompilerParams(vmem_limit_bytes=16 << 20),
        name="factor",
    )(own, other)


def sum_devices(mine, other, scale):
    planes = lax.axis_size("y") * lax.axis_size("z")
    groups = lax.axis_size("x")
    shape = mine.shape
    swap = [(0, 1), (1, 0)]
    mine = mine + lax.ppermute(other, "core", swap)
    pieces = lax.all_to_all(mine.reshape(planes, -1, 128), PLANE, 0, 0)
    piece = jnp.sum(pieces, axis=0)
    for k in (1, 2):
        piece = piece + lax.ppermute(piece, "x", [(i, i ^ k) for i in range(groups)])
    whole = lax.all_to_all(jnp.broadcast_to(piece * scale, pieces.shape), PLANE, 0, 0).reshape(shape)
    return whole, lax.ppermute(whole, "core", swap)


def program(cam_disp, footprint, stencil, frac, coef):
    cam_count, pix, snaps = cam_disp.shape[2], cam_disp.shape[4], cam_disp.shape[5]
    world_tiles = footprint.shape[2]
    cells = coef.shape[-1]
    groups = lax.axis_size("x")
    tiles = cam_disp.reshape(cam_count, 2, pix, snaps)
    tiles = pltpu.with_memory_space_constraint(tiles, pltpu.HBM)
    ids = footprint.reshape(world_tiles, 2)

    swaps = [[(i, i ^ k) for i in range(groups)] for k in range(groups)]
    ids, sent = early(ids, tiles)
    asked, firsts = [None], []
    for k in range(1, groups):
        asked.append(lax.ppermute(ids, "x", swaps[k]))
    for k in range(1, groups):
        firsts.append(lax.ppermute(sent, "x", swaps[k]))
    received = [[None] * groups for _ in range(world_tiles)]
    for k in range(1, groups):
        payload = select(asked[k], tiles)
        for w in range(world_tiles):
            received[w][k] = lax.ppermute(payload[w], "x", swaps[k])

    mats, columns = prepare(
        stencil.reshape(world_tiles * 2, 2, cells),
        frac.reshape(world_tiles * 2, 2, cells),
        coef.reshape(world_tiles, 12, cells),
        pix,
    )

    carry = None
    for w in range(world_tiles):
        carry = world(w, ids, tiles, firsts, received[w][1:], mats, columns, carry)
    velocity, mine, other = carry
    total_rows = groups * lax.axis_size("y") * lax.axis_size("z") * 2 * world_tiles * 3 * cells
    halves = sum_devices(mine, other, F32(1.0 / total_rows))
    return (velocity.reshape(1, 1, world_tiles, 3, cells, snaps), factor(*halves, snaps))


def solution(mesh):
    grid = Mesh(mesh.devices.reshape(4, 4, 2, 4), ("y", "z", "core", "x"))
    columns = ("y", "z", "core")
    in_specs = (
        P("x", columns, None, None, None, None),
        P("x", columns, None, None),
        P("x", columns, None, None, None, None),
        P("x", columns, None, None, None, None),
        P("x", columns, None, None, None, None),
    )
    out_specs = (P("x", columns, None, None, None, None), P())
    return jax.shard_map(program, mesh=grid, in_specs=in_specs, out_specs=out_specs, check_vma=False)
```

profile of v0, /device:TPU:1, one launch (start us, length us, event | category | flops | bytes accessed | tf_op | source)
XLA Modules:
  0.0 142.2 jit_solution(18008721022522133504)
XLA Ops:
  0.6 0.0 copy-start.2
  0.6 0.7 copy-done.2
  1.3 1.0 early.1
  2.3 2.1 %collective-permute-start.3 = (s32[2,2]{1,0:T(2,128)S(1)}, s32[2,2]{1,0:T(2,128)S(1)}, u32[]{:S(2)}, u32[]{:S(2)}) collective-permute-start(s32[2,2]{1,0:T(2,128)S(1)} %get-tuple-element.17.ids_ref), channel_id=1, source_target_pairs={{0,1},{1,0},{2,3},{3,2},{4,5},{5,4},{6,7},{7,6},{8,9},{9,8},{10,11... | collective-permute-start | bytes 56 | tf_op jit(solution)/shard_map/ppermute | solution.py:357
  4.4 1.0 collective-permute-done.3.ids_ref
  5.4 1.7 %shard_map.68 = (bf16[2,224,512]{2,1,0:T(8,128)(2,1)S(1)}, bf16[2,224,512]{2,1,0:T(8,128)(2,1)S(1)}) custom-call(s32[2,2]{1,0:T(2,128)S(1)} %collective-permute-done.3.ids_ref, bf16[4,2,256,512]{3,2,1,0:T(8,128)(2,1)} %bitcast.14), custom_call_target="tpu_custom_call" | custom-call | bytes 2000000 | tf_op jit(solution)/shard_map/pallas_call | solution.py:115
  7.1 1.5 %collective-permute-start.9 = (bf16[2,224,512]{2,1,0:T(8,128)(2,1)S(1)}, bf16[2,224,512]{2,1,0:T(8,128)(2,1)S(1)}, u32[]{:S(2)}, u32[]{:S(2)}) collective-permute-start(bf16[2,224,512]{2,1,0:T(8,128)(2,1)S(1)} %get-tuple-element.24), channel_id=1, source_target_pairs={{0,1},{1,0},{2,3},{3,2},{4,5},{5,4},{6,7},{7,6},{8,9},{9,8},{10,11... | collective-permute-start | bytes 1376264 | tf_op jit(solution)/shard_map/ppermute | solution.py:364
  8.6 1.8 %collective-permute-start.2 = (bf16[4,2,32,512]{3,2,1,0:T(8,128)(2,1)S(1)}, bf16[4,2,32,512]{3,2,1,0:T(8,128)(2,1)S(1)}, u32[]{:S(2)}, u32[]{:S(2)}) collective-permute-start(bf16[4,2,32,512]{3,2,1,0:T(8,128)(2,1)S(1)} %get-tuple-element.18), channel_id=1, source_target_pairs={{0,3},{1,2},{2,1},{3,0},{4,7},{5,6},{6,5},{7,4},{8,11},{9,10},{10,... | collective-permute-start | bytes 786440 | tf_op jit(solution)/shard_map/ppermute | solution.py:359
  10.5 0.6 collective-permute-start.1
  11.1 0.8 collective-permute-start
  11.9 2.5 %collective-permute-start.5 = (s32[2,2]{1,0:T(2,128)S(1)}, s32[2,2]{1,0:T(2,128)S(1)}, u32[]{:S(2)}, u32[]{:S(2)}) collective-permute-start(s32[2,2]{1,0:T(2,128)S(1)} %get-tuple-element.17.ids_ref), channel_id=1, source_target_pairs={{0,2},{1,3},{2,0},{3,1},{4,6},{5,7},{6,4},{7,5},{8,10},{9,11},{10,... | collective-permute-start | bytes 56 | tf_op jit(solution)/shard_map/ppermute | solution.py:357
  14.3 16.4 %collective-permute-done.5.ids_ref = s32[2,2]{1,0:T(2,128)S(1)} collective-permute-done((s32[2,2]{1,0:T(2,128)S(1)}, s32[2,2]{1,0:T(2,128)S(1)}, u32[]{:S(2)}, u32[]{:S(2)}) %collective-permute-start.5) | collective-permute-done | bytes 48 | tf_op jit(solution)/shard_map/ppermute | solution.py:357
  30.7 0.0 collective-permute-start.7
  30.7 1.7 %shard_map.69 = (bf16[2,224,512]{2,1,0:T(8,128)(2,1)S(1)}, bf16[2,224,512]{2,1,0:T(8,128)(2,1)S(1)}) custom-call(s32[2,2]{1,0:T(2,128)S(1)} %collective-permute-done.5.ids_ref, bf16[4,2,256,512]{3,2,1,0:T(8,128)(2,1)} %bitcast.15), custom_call_target="tpu_custom_call" | custom-call | bytes 2000000 | tf_op jit(solution)/shard_map/pallas_call | solution.py:115
  32.5 0.0 copy-start.3
  32.5 0.0 copy-start
  32.5 0.0 copy-start.1
  32.5 1.9 %collective-permute-done.7.ids_ref = s32[2,2]{1,0:T(2,128)S(1)} collective-permute-done((s32[2,2]{1,0:T(2,128)S(1)}, s32[2,2]{1,0:T(2,128)S(1)}, u32[]{:S(2)}, u32[]{:S(2)}) %collective-permute-start.7) | collective-permute-done | bytes 48 | tf_op jit(solution)/shard_map/ppermute | solution.py:357
  34.4 0.1 collective-permute-start.10
  34.4 1.7 %shard_map.70 = (bf16[2,224,512]{2,1,0:T(8,128)(2,1)S(1)}, bf16[2,224,512]{2,1,0:T(8,128)(2,1)S(1)}) custom-call(s32[2,2]{1,0:T(2,128)S(1)} %collective-permute-done.7.ids_ref, bf16[4,2,256,512]{3,2,1,0:T(8,128)(2,1)} %bitcast.16), custom_call_target="tpu_custom_call" | custom-call | bytes 2000000 | tf_op jit(solution)/shard_map/pallas_call | solution.py:115
  36.2 0.0 collective-permute-done.2.e3_ref
  36.2 1.4 collective-permute-start.11
  37.6 0.0 collective-permute-done.1.e2_ref
  37.6 1.3 collective-permute-start.4
  38.8 0.0 collective-permute-done.e1_ref
  38.9 1.3 collective-permute-start.6
  40.1 0.0 collective-permute-done.9.r1_ref
  40.1 1.3 collective-permute-start.8
  41.5 0.0 copy-done.3
  41.5 0.0 copy-done
  41.5 0.0 copy-done.1
  41.5 1.9 %prepare.1 = (bf16[2,2,256,256]{3,2,1,0:T(8,128)(2,1)S(1)}, f32[256,128]{1,0:T(8,128)S(1)}) custom-call(s32[4,2,256]{2,1,0:T(2,128)S(1)} %bitcast.10, f32[4,2,256]{2,1,0:T(2,128)S(1)} %bitcast.11, f32[2,12,256]{2,1,0:T(8,128)S(1)} %copy.9.coef_ref), custom_call_target="tpu_custom_call" | custom-call | flops 4000000 | bytes 1000000 | tf_op jit(solution)/shard_map/prepare/pallas_call | solution.py:60
  43.4 0.4 collective-permute-done.10.r2_ref
  43.8 17.9 %collective-permute-done.11.r3_ref = bf16[2,224,512]{2,1,0:T(8,128)(2,1)S(1)} collective-permute-done((bf16[2,224,512]{2,1,0:T(8,128)(2,1)S(1)}, bf16[2,224,512]{2,1,0:T(8,128)(2,1)S(1)}, u32[]{:S(2)}, u32[]{:S(2)}) %collective-permute-start.11) | collective-permute-done | bytes 458784 | tf_op jit(solution)/shard_map/ppermute | solution.py:364
  61.7 3.4 %shard_map.71 = (bf16[2,3,256,512]{3,2,1,0:T(8,128)(2,1)}, f32[2,5,128,128]{3,2,1,0:T(8,128)S(1)}) custom-call(s32[2,2]{1,0:T(2,128)S(1)} %get-tuple-element.17.ids_ref, bf16[4,2,256,512]{3,2,1,0:T(8,128)(2,1)} %bitcast.17, bf16[4,2,32,512]{3,2,1,0:T(8,128)(2,1)S(1)} %collective-permute-done.e1_ref, ...), custom_call_target="tpu_custom_call" | custom-call | flops 700000000 | bytes 4000000 | tf_op jit(solution)/shard_map/pallas_call | solution.py:208
  65.1 0.0 collective-permute-done.4.r1_ref
  65.1 0.0 collective-permute-done.6.r2_ref
  65.1 12.2 %collective-permute-done.8.r3_ref = bf16[2,224,512]{2,1,0:T(8,128)(2,1)S(1)} collective-permute-done((bf16[2,224,512]{2,1,0:T(8,128)(2,1)S(1)}, bf16[2,224,512]{2,1,0:T(8,128)(2,1)S(1)}, u32[]{:S(2)}, u32[]{:S(2)}) %collective-permute-start.8) | collective-permute-done | bytes 458784 | tf_op jit(solution)/shard_map/ppermute | solution.py:364
  77.3 4.2 %shard_map.72 = (bf16[2,3,256,512]{3,2,1,0:T(8,128)(2,1)}, f32[5,128,128]{2,1,0:T(8,128)S(1)}, f32[5,128,128]{2,1,0:T(8,128)S(1)}) custom-call(s32[2,2]{1,0:T(2,128)S(1)} %get-tuple-element.17.ids_ref, bf16[4,2,256,512]{3,2,1,0:T(8,128)(2,1)} %bitcast.18, bf16[4,2,32,512]{3,2,1,0:T(8,128)(2,1)S(1)} %collective-permute-done.e1_ref, ...), custom_call_target="tpu_custom_call", output_to_operand_aliasing={{0}: (11, {})} | custom-call | flops 700000000 | bytes 4000000 | tf_op jit(solution)/shard_map/pallas_call | solution.py:208
  81.5 1.6 %collective-permute-start.12 = (f32[5,128,128]{2,1,0:T(8,128)S(1)}, f32[5,128,128]{2,1,0:T(8,128)S(1)}, u32[]{:S(2)}, u32[]{:S(2)}) collective-permute-start(f32[5,128,128]{2,1,0:T(8,128)S(1)} %get-tuple-element.31), channel_id=1, source_target_pairs={{0,4},{4,0},{1,5},{5,1},{2,6},{6,2},{3,7},{7,3},{8,12},{12,8},{9,1... | collective-permute-start | bytes 983048 | tf_op jit(solution)/shard_map/ppermute | solution.py:335
  83.1 1.3 collective-permute-done.12
  84.4 15.1 %all_to_all.10 = f32[16,40,128]{2,1,0:T(8,128)S(1)} all-to-all(f32[16,40,128]{2,1,0:T(8,128)S(1)} %bitcast.20), channel_id=1, replica_groups=mesh['y'=4,'z'=4,'core'=2,'x'=4] {'y','z'}, dimensions={0} | all-to-all | bytes 655360 | tf_op jit(solution)/shard_map/all_to_all | solution.py:336
  99.5 0.1 collective-permute-start.13
  99.6 2.6 %collective-permute-done.13 = f32[40,128]{1,0:T(8,128)S(1)} collective-permute-done((f32[40,128]{1,0:T(8,128)S(1)}, f32[40,128]{1,0:T(8,128)S(1)}, u32[]{:S(2)}, u32[]{:S(2)}) %collective-permute-start.13) | collective-permute-done | bytes 20512 | tf_op jit(solution)/shard_map/ppermute | solution.py:339
  102.2 1.6 %collective-permute-start.14 = (f32[40,128]{1,0:T(8,128)S(1)}, f32[40,128]{1,0:T(8,128)S(1)}, u32[]{:S(2)}, u32[]{:S(2)}) collective-permute-start(f32[40,128]{1,0:T(8,128)S(1)} %add.10), channel_id=1, source_target_pairs={{0,2},{1,3},{2,0},{3,1},{4,6},{5,7},{6,4},{7,5},{8,10},{9,11},{10,... | collective-permute-start | bytes 61448 | tf_op jit(solution)/shard_map/ppermute | solution.py:339
  103.8 2.6 %collective-permute-done.14 = f32[40,128]{1,0:T(8,128)S(1)} collective-permute-done((f32[40,128]{1,0:T(8,128)S(1)}, f32[40,128]{1,0:T(8,128)S(1)}, u32[]{:S(2)}, u32[]{:S(2)}) %collective-permute-start.14) | collective-permute-done | bytes 20512 | tf_op jit(solution)/shard_map/ppermute | solution.py:339
  106.5 11.4 %all_to_all.11 = f32[16,40,128]{2,1,0:T(8,128)S(1)} all-to-all(f32[16,40,128]{2,1,0:T(8,128)S(1)} %broadcast_in_dim.3), channel_id=1, replica_groups=mesh['y'=4,'z'=4,'core'=2,'x'=4] {'y','z'}, dimensions={0} | all-to-all | bytes 655360 | tf_op jit(solution)/shard_map/all_to_all | solution.py:340
  117.9 5.2 %collective-permute-start.15 = (f32[5,128,128]{2,1,0:T(8,128)S(1)}, f32[5,128,128]{2,1,0:T(8,128)S(1)}, u32[]{:S(2)}, u32[]{:S(2)}) collective-permute-start(f32[5,128,128]{2,1,0:T(8,128)S(1)} %bitcast.8), channel_id=1, source_target_pairs={{0,4},{4,0},{1,5},{5,1},{2,6},{6,2},{3,7},{7,3},{8,12},{12,8},{9,1... | collective-permute-start | bytes 983048 | tf_op jit(solution)/shard_map/ppermute | solution.py:341
  123.1 1.3 collective-permute-done.15.other_ref
  124.4 17.8 %factor.1 = f32[512,512]{1,0:T(8,128)} custom-call(f32[5,128,128]{2,1,0:T(8,128)S(1)} %bitcast.9, f32[5,128,128]{2,1,0:T(8,128)S(1)} %collective-permute-done.15.other_ref), custom_call_target="tpu_custom_call" | custom-call | tf_op jit(solution)/shard_map/factor/pallas_call | solution.py:319
  (7 shorter events, 0.1 us)
Async XLA Ops:
  0.6 0.7 copy-start.2
  2.3 3.1 %collective-permute-start.3 = (s32[2,2]{1,0:T(2,128)S(1)}, s32[2,2]{1,0:T(2,128)S(1)}, u32[]{:S(2)}, u32[]{:S(2)}) collective-permute-start(s32[2,2]{1,0:T(2,128)S(1)} %get-tuple-element.17.ids_ref), channel_id=1, source_target_pairs={{0,1},{1,0},{2,3},{3,2},{4,5},{5,4},{6,7},{7,6},{8,9},{9,8},{10,11... | collective-permute-start | bytes 56 | tf_op jit(solution)/shard_map/ppermute | solution.py:357
  7.1 33.0 %collective-permute-start.9 = (bf16[2,224,512]{2,1,0:T(8,128)(2,1)S(1)}, bf16[2,224,512]{2,1,0:T(8,128)(2,1)S(1)}, u32[]{:S(2)}, u32[]{:S(2)}) collective-permute-start(bf16[2,224,512]{2,1,0:T(8,128)(2,1)S(1)} %get-tuple-element.24), channel_id=1, source_target_pairs={{0,1},{1,0},{2,3},{3,2},{4,5},{5,4},{6,7},{7,6},{8,9},{9,8},{10,11... | collective-permute-start | bytes 1376264 | tf_op jit(solution)/shard_map/ppermute | solution.py:364
  8.6 27.5 %collective-permute-start.2 = (bf16[4,2,32,512]{3,2,1,0:T(8,128)(2,1)S(1)}, bf16[4,2,32,512]{3,2,1,0:T(8,128)(2,1)S(1)}, u32[]{:S(2)}, u32[]{:S(2)}) collective-permute-start(bf16[4,2,32,512]{3,2,1,0:T(8,128)(2,1)S(1)} %get-tuple-element.18), channel_id=1, source_target_pairs={{0,3},{1,2},{2,1},{3,0},{4,7},{5,6},{6,5},{7,4},{8,11},{9,10},{10,... | collective-permute-start | bytes 786440 | tf_op jit(solution)/shard_map/ppermute | solution.py:359
  10.5 27.1 %collective-permute-start.1 = (bf16[4,2,32,512]{3,2,1,0:T(8,128)(2,1)S(1)}, bf16[4,2,32,512]{3,2,1,0:T(8,128)(2,1)S(1)}, u32[]{:S(2)}, u32[]{:S(2)}) collective-permute-start(bf16[4,2,32,512]{3,2,1,0:T(8,128)(2,1)S(1)} %get-tuple-element.18), channel_id=1, source_target_pairs={{0,2},{1,3},{2,0},{3,1},{4,6},{5,7},{6,4},{7,5},{8,10},{9,11},{10,... | collective-permute-start | bytes 786440 | tf_op jit(solution)/shard_map/ppermute | solution.py:359
  11.1 27.8 %collective-permute-start = (bf16[4,2,32,512]{3,2,1,0:T(8,128)(2,1)S(1)}, bf16[4,2,32,512]{3,2,1,0:T(8,128)(2,1)S(1)}, u32[]{:S(2)}, u32[]{:S(2)}) collective-permute-start(bf16[4,2,32,512]{3,2,1,0:T(8,128)(2,1)S(1)} %get-tuple-element.18), channel_id=1, source_target_pairs={{0,1},{1,0},{2,3},{3,2},{4,5},{5,4},{6,7},{7,6},{8,9},{9,8},{10,11... | collective-permute-start | bytes 786440 | tf_op jit(solution)/shard_map/ppermute | solution.py:359
  11.9 18.8 %collective-permute-start.5 = (s32[2,2]{1,0:T(2,128)S(1)}, s32[2,2]{1,0:T(2,128)S(1)}, u32[]{:S(2)}, u32[]{:S(2)}) collective-permute-start(s32[2,2]{1,0:T(2,128)S(1)} %get-tuple-element.17.ids_ref), channel_id=1, source_target_pairs={{0,2},{1,3},{2,0},{3,1},{4,6},{5,7},{6,4},{7,5},{8,10},{9,11},{10,... | collective-permute-start | bytes 56 | tf_op jit(solution)/shard_map/ppermute | solution.py:357
  30.7 3.6 %collective-permute-start.7 = (s32[2,2]{1,0:T(2,128)S(1)}, s32[2,2]{1,0:T(2,128)S(1)}, u32[]{:S(2)}, u32[]{:S(2)}) collective-permute-start(s32[2,2]{1,0:T(2,128)S(1)} %get-tuple-element.17.ids_ref), channel_id=1, source_target_pairs={{0,3},{1,2},{2,1},{3,0},{4,7},{5,6},{6,5},{7,4},{8,11},{9,10},{10,... | collective-permute-start | bytes 56 | tf_op jit(solution)/shard_map/ppermute | solution.py:357
  32.5 9.0 %copy-start.3 = (f32[1,1,2,3,4,256]{5,4,3,2,1,0:T(4,128)S(1)}, f32[1,1,2,3,4,256]{5,4,3,2,1,0:T(4,128)}, u32[]{:S(2)}) copy-start(f32[1,1,2,3,4,256]{5,4,3,2,1,0:T(4,128)} %param.9) | copy-start | bytes 73732
  32.5 9.0 %copy-start = (s32[1,1,2,2,2,256]{5,4,3,2,1,0:T(2,128)S(1)}, s32[1,1,2,2,2,256]{5,4,3,2,1,0:T(2,128)}, u32[]{:S(2)}) copy-start(s32[1,1,2,2,2,256]{5,4,3,2,1,0:T(2,128)} %param.7) | copy-start | bytes 24580
  32.5 9.0 %copy-start.1 = (f32[1,1,2,2,2,256]{5,4,3,2,1,0:T(2,128)S(1)}, f32[1,1,2,2,2,256]{5,4,3,2,1,0:T(2,128)}, u32[]{:S(2)}) copy-start(f32[1,1,2,2,2,256]{5,4,3,2,1,0:T(2,128)} %param.8) | copy-start | bytes 24580
  34.4 9.4 %collective-permute-start.10 = (bf16[2,224,512]{2,1,0:T(8,128)(2,1)S(1)}, bf16[2,224,512]{2,1,0:T(8,128)(2,1)S(1)}, u32[]{:S(2)}, u32[]{:S(2)}) collective-permute-start(bf16[2,224,512]{2,1,0:T(8,128)(2,1)S(1)} %get-tuple-element.25), channel_id=1, source_target_pairs={{0,2},{1,3},{2,0},{3,1},{4,6},{5,7},{6,4},{7,5},{8,10},{9,11},{10,... | collective-permute-start | bytes 1376264 | tf_op jit(solution)/shard_map/ppermute | solution.py:364
  36.2 25.6 %collective-permute-start.11 = (bf16[2,224,512]{2,1,0:T(8,128)(2,1)S(1)}, bf16[2,224,512]{2,1,0:T(8,128)(2,1)S(1)}, u32[]{:S(2)}, u32[]{:S(2)}) collective-permute-start(bf16[2,224,512]{2,1,0:T(8,128)(2,1)S(1)} %get-tuple-element.26), channel_id=1, source_target_pairs={{0,3},{1,2},{2,1},{3,0},{4,7},{5,6},{6,5},{7,4},{8,11},{9,10},{10,... | collective-permute-start | bytes 1376264 | tf_op jit(solution)/shard_map/ppermute | solution.py:364
  37.6 27.5 %collective-permute-start.4 = (bf16[2,224,512]{2,1,0:T(8,128)(2,1)S(1)}, bf16[2,224,512]{2,1,0:T(8,128)(2,1)S(1)}, u32[]{:S(2)}, u32[]{:S(2)}) collective-permute-start(bf16[2,224,512]{2,1,0:T(8,128)(2,1)S(1)} %get-tuple-element.19), channel_id=1, source_target_pairs={{0,1},{1,0},{2,3},{3,2},{4,5},{5,4},{6,7},{7,6},{8,9},{9,8},{10,11... | collective-permute-start | bytes 1376264 | tf_op jit(solution)/shard_map/ppermute | solution.py:364
  38.9 26.3 %collective-permute-start.6 = (bf16[2,224,512]{2,1,0:T(8,128)(2,1)S(1)}, bf16[2,224,512]{2,1,0:T(8,128)(2,1)S(1)}, u32[]{:S(2)}, u32[]{:S(2)}) collective-permute-start(bf16[2,224,512]{2,1,0:T(8,128)(2,1)S(1)} %get-tuple-element.20), channel_id=1, source_target_pairs={{0,2},{1,3},{2,0},{3,1},{4,6},{5,7},{6,4},{7,5},{8,10},{9,11},{10,... | collective-permute-start | bytes 1376264 | tf_op jit(solution)/shard_map/ppermute | solution.py:364
  40.1 37.2 %collective-permute-start.8 = (bf16[2,224,512]{2,1,0:T(8,128)(2,1)S(1)}, bf16[2,224,512]{2,1,0:T(8,128)(2,1)S(1)}, u32[]{:S(2)}, u32[]{:S(2)}) collective-permute-start(bf16[2,224,512]{2,1,0:T(8,128)(2,1)S(1)} %get-tuple-element.21), channel_id=1, source_target_pairs={{0,3},{1,2},{2,1},{3,0},{4,7},{5,6},{6,5},{7,4},{8,11},{9,10},{10,... | collective-permute-start | bytes 1376264 | tf_op jit(solution)/shard_map/ppermute | solution.py:364
  81.5 2.8 %collective-permute-start.12 = (f32[5,128,128]{2,1,0:T(8,128)S(1)}, f32[5,128,128]{2,1,0:T(8,128)S(1)}, u32[]{:S(2)}, u32[]{:S(2)}) collective-permute-start(f32[5,128,128]{2,1,0:T(8,128)S(1)} %get-tuple-element.31), channel_id=1, source_target_pairs={{0,4},{4,0},{1,5},{5,1},{2,6},{6,2},{3,7},{7,3},{8,12},{12,8},{9,1... | collective-permute-start | bytes 983048 | tf_op jit(solution)/shard_map/ppermute | solution.py:335
  99.5 2.7 %collective-permute-start.13 = (f32[40,128]{1,0:T(8,128)S(1)}, f32[40,128]{1,0:T(8,128)S(1)}, u32[]{:S(2)}, u32[]{:S(2)}) collective-permute-start(f32[40,128]{1,0:T(8,128)S(1)} %reduce_sum.9), channel_id=1, source_target_pairs={{0,1},{1,0},{2,3},{3,2},{4,5},{5,4},{6,7},{7,6},{8,9},{9,8},{10,11... | collective-permute-start | bytes 61448 | tf_op jit(solution)/shard_map/ppermute | solution.py:339
  102.2 4.3 %collective-permute-start.14 = (f32[40,128]{1,0:T(8,128)S(1)}, f32[40,128]{1,0:T(8,128)S(1)}, u32[]{:S(2)}, u32[]{:S(2)}) collective-permute-start(f32[40,128]{1,0:T(8,128)S(1)} %add.10), channel_id=1, source_target_pairs={{0,2},{1,3},{2,0},{3,1},{4,6},{5,7},{6,4},{7,5},{8,10},{9,11},{10,... | collective-permute-start | bytes 61448 | tf_op jit(solution)/shard_map/ppermute | solution.py:339
  117.9 6.5 %collective-permute-start.15 = (f32[5,128,128]{2,1,0:T(8,128)S(1)}, f32[5,128,128]{2,1,0:T(8,128)S(1)}, u32[]{:S(2)}, u32[]{:S(2)}) collective-permute-start(f32[5,128,128]{2,1,0:T(8,128)S(1)} %bitcast.8), channel_id=1, source_target_pairs={{0,4},{4,0},{1,5},{5,1},{2,6},{6,2},{3,7},{7,3},{8,12},{12,8},{9,1... | collective-permute-start | bytes 983048 | tf_op jit(solution)/shard_map/ppermute | solution.py:341
where the time goes:
time: 143 us; the launch traced here: 142 us
  waiting for transfers between devices  57.6 us (40%)
  Pallas kernels  33.3 us (23%)
  blocking collectives  26.5 us (19%)
  starting transfers between devices  23.2 us (16%)
    ppermute x6, waiting for transfers between devices, program(): received[w][k] = lax.ppermute(payload[w], 'x', swaps[k])  30.6 us
    ppermute x3, waiting for transfers between devices, program(): asked.append(lax.ppermute(ids, 'x', swaps[k]))  19.2 us
    pallas_call x1, Pallas kernels, factor(): pl.pallas_call(factor_kernel, out_shape=jax.ShapeDtypeStruct((n, n), F32)...  17.8 us
    all_to_all x1, blocking collectives, sum_devices(): pieces = lax.all_to_all(mine.reshape(planes, -1, 128), PLANE, 0, 0)  15.1 us
    all_to_all x1, blocking collectives, sum_devices(): lax.all_to_all(jnp.broadcast_to(piece * scale, pieces.shape), PLANE, 0, 0)  11.4 us
    pallas_call x2, Pallas kernels, world(): pl.pallas_call(functools.partial(world_kernel, w), grid=(1,), in_specs=in...  7.54 us
    ppermute x6, starting transfers between devices, program(): received[w][k] = lax.ppermute(payload[w], 'x', swaps[k])  6.87 us
    ppermute x2, waiting for transfers between devices, sum_devices(): lax.ppermute(piece, 'x', [(i, i ^ k) for i in range(groups)])  5.25 us
  transfers between devices with their start and end apart: 16, of which 10 were waited for; matrix products, arithmetic and copies ran while one was open for 0% of the time, Pallas kernels for 6%

commit v1 on v0

--- a/solution.py
+++ b/solution.py
@@ -71,13 +71,15 @@
     )(sten, frac, coef)
 
 
-def early_kernel(ids_ref, cam_ref, ids_out, out, sem):
+def early_kernel(ids_ref, cam_ref, ids_out, out, sem, ids_sem):
     copies = [pltpu.make_async_copy(cam_ref.at[t, :, pl.ds(0, EARLY)], out.at[t], sem.at[t]) for t in range(cam_ref.shape[0])]
     for copy in copies:
         copy.start()
-    ids_out[...] = ids_ref[...]
+    ids_copy = pltpu.make_async_copy(ids_ref, ids_out, ids_sem)
+    ids_copy.start()
     for copy in copies:
         copy.wait()
+    ids_copy.wait()
 
 
 def early(ids, tiles):
@@ -85,9 +87,9 @@
     return pl.pallas_call(
         early_kernel,
         out_shape=[jax.ShapeDtypeStruct(ids.shape, ids.dtype), jax.ShapeDtypeStruct((count, parts, EARLY, snaps), tiles.dtype)],
-        in_specs=[VM, ANY],
+        in_specs=[ANY, ANY],
         out_specs=[VM, VM],
-        scratch_shapes=[pltpu.SemaphoreType.DMA((count,))],
+        scratch_shapes=[pltpu.SemaphoreType.DMA((count,)), pltpu.SemaphoreType.DMA],
         compiler_params=pltpu.CompilerParams(vmem_limit_bytes=4 << 20),
         cost_estimate=pl.CostEstimate(flops=0, bytes_accessed=500_000, transcendentals=0),
         name="early",
@@ -247,20 +249,19 @@
         scaled = [None] * per
         for k in range(size):
             at, here = k // 8, is_row[k % 8]
+
+            def fill(parts, value):
+                return [jnp.where(here, value, x) if v == at else x for v, x in enumerate(parts)]
+
+            pivot, row = fill(columns[k], -1.0), spread(rows[at], k)
             root = lax.rsqrt(spread(columns[k][at], k))
-            inverse = root * root
-            row = spread(rows[at], k)
+            pivot = [x * root for x in pivot]
             final = row * root
             scaled[at] = final if scaled[at] is None else jnp.where(here, final, scaled[at])
-            t = row * inverse
             for j in range(k + 1, size):
-                ct = spread(columns[j][at], k) * inverse
-                new = [columns[j][v] - columns[k][v] * ct for v in range(per)]
-                new[at] = jnp.where(here, ct, new[at])
-                columns[j] = new
-            new = [rows[v] - columns[k][v] * t for v in range(per)]
-            new[at] = jnp.where(here, t, new[at])
-            rows = new
+                ct = spread(columns[j][at], k) * root
+                columns[j] = [x - pivot[v] * ct for v, x in enumerate(fill(columns[j], 0.0))]
+            rows = [x - pivot[v] * final for v, x in enumerate(fill(rows, 0.0))]
         out.extend(jnp.where(lane < k0 + size, x, 0.0) for x in scaled)
         solved = [spread(rows[k // 8], k) for k in range(size)]
         for b in range((s + 1) * per, len(blocks)):
@@ -348,7 +349,7 @@
     groups = lax.axis_size("x")
     tiles = cam_disp.reshape(cam_count, 2, pix, snaps)
     tiles = pltpu.with_memory_space_constraint(tiles, pltpu.HBM)
-    ids = footprint.reshape(world_tiles, 2)
+    ids = pltpu.with_memory_space_constraint(footprint.reshape(world_tiles, 2), pltpu.HBM)
 
     swaps = [[(i, i ^ k) for i in range(groups)] for k in range(groups)]
     ids, sent = early(ids, tiles)

time: 143 us -> 140 us (0.979)
  no operation moved by 1% of the time
where the time goes in v1:
time: 140 us
  waiting for transfers between devices  57.6 us (41%)
  Pallas kernels  31.9 us (23%)
  blocking collectives  26.5 us (19%)
  starting transfers between devices  23.2 us (17%)
    ppermute x6, waiting for transfers between devices, program(): received[w][k] = lax.ppermute(payload[w], 'x', swaps[k])  30.6 us
    ppermute x3, waiting for transfers between devices, program(): asked.append(lax.ppermute(ids, 'x', swaps[k]))  19.2 us
    pallas_call x1, Pallas kernels, factor(): pl.pallas_call(factor_kernel, out_shape=jax.ShapeDtypeStruct((n, n), F32)...  16.4 us
    all_to_all x1, blocking collectives, sum_devices(): pieces = lax.all_to_all(mine.reshape(planes, -1, 128), PLANE, 0, 0)  15.1 us
    all_to_all x1, blocking collectives, sum_devices(): lax.all_to_all(jnp.broadcast_to(piece * scale, pieces.shape), PLANE, 0, 0)  11.4 us
    pallas_call x2, Pallas kernels, world(): pl.pallas_call(functools.partial(world_kernel, w), grid=(1,), in_specs=in...  7.54 us
    ppermute x6, starting transfers between devices, program(): received[w][k] = lax.ppermute(payload[w], 'x', swaps[k])  6.87 us
    ppermute x2, waiting for transfers between devices, sum_devices(): lax.ppermute(piece, 'x', [(i, i ^ k) for i in range(groups)])  5.25 us
  transfers between devices with their start and end apart: 16, of which 10 were waited for; matrix products, arithmetic and copies ran while one was open for 0% of the time, Pallas kernels for 6%

profile of v1, /device:TPU:1, one launch (start us, length us, event | category | flops | bytes accessed | tf_op | source)
XLA Modules:
  0.0 140.1 jit_solution(3956675355978919538)
XLA Ops:
  0.6 1.0 early.1
  1.6 2.1 %collective-permute-start.3 = (s32[2,2]{1,0:T(2,128)S(1)}, s32[2,2]{1,0:T(2,128)S(1)}, u32[]{:S(2)}, u32[]{:S(2)}) collective-permute-start(s32[2,2]{1,0:T(2,128)S(1)} %get-tuple-element.17.ids_ref), channel_id=1, source_target_pairs={{0,1},{1,0},{2,3},{3,2},{4,5},{5,4},{6,7},{7,6},{8,9},{9,8},{10,11... | collective-permute-start | bytes 56 | tf_op jit(solution)/shard_map/ppermute | solution.py:358
  3.7 1.0 collective-permute-done.3.ids_ref
  4.7 1.7 %shard_map.68 = (bf16[2,224,512]{2,1,0:T(8,128)(2,1)S(1)}, bf16[2,224,512]{2,1,0:T(8,128)(2,1)S(1)}) custom-call(s32[2,2]{1,0:T(2,128)S(1)} %collective-permute-done.3.ids_ref, bf16[4,2,256,512]{3,2,1,0:T(8,128)(2,1)} %bitcast.13), custom_call_target="tpu_custom_call" | custom-call | bytes 2000000 | tf_op jit(solution)/shard_map/pallas_call | solution.py:117
  6.4 1.5 %collective-permute-start.9 = (bf16[2,224,512]{2,1,0:T(8,128)(2,1)S(1)}, bf16[2,224,512]{2,1,0:T(8,128)(2,1)S(1)}, u32[]{:S(2)}, u32[]{:S(2)}) collective-permute-start(bf16[2,224,512]{2,1,0:T(8,128)(2,1)S(1)} %get-tuple-element.24), channel_id=1, source_target_pairs={{0,1},{1,0},{2,3},{3,2},{4,5},{5,4},{6,7},{7,6},{8,9},{9,8},{10,11... | collective-permute-start | bytes 1376264 | tf_op jit(solution)/shard_map/ppermute | solution.py:365
  8.0 1.8 %collective-permute-start.2 = (bf16[4,2,32,512]{3,2,1,0:T(8,128)(2,1)S(1)}, bf16[4,2,32,512]{3,2,1,0:T(8,128)(2,1)S(1)}, u32[]{:S(2)}, u32[]{:S(2)}) collective-permute-start(bf16[4,2,32,512]{3,2,1,0:T(8,128)(2,1)S(1)} %get-tuple-element.18), channel_id=1, source_target_pairs={{0,3},{1,2},{2,1},{3,0},{4,7},{5,6},{6,5},{7,4},{8,11},{9,10},{10,... | collective-permute-start | bytes 786440 | tf_op jit(solution)/shard_map/ppermute | solution.py:360
  9.8 0.6 collective-permute-start.1
  10.4 0.8 collective-permute-start
  11.2 2.5 %collective-permute-start.5 = (s32[2,2]{1,0:T(2,128)S(1)}, s32[2,2]{1,0:T(2,128)S(1)}, u32[]{:S(2)}, u32[]{:S(2)}) collective-permute-start(s32[2,2]{1,0:T(2,128)S(1)} %get-tuple-element.17.ids_ref), channel_id=1, source_target_pairs={{0,2},{1,3},{2,0},{3,1},{4,6},{5,7},{6,4},{7,5},{8,10},{9,11},{10,... | collective-permute-start | bytes 56 | tf_op jit(solution)/shard_map/ppermute | solution.py:358
  13.7 16.4 %collective-permute-done.5.ids_ref = s32[2,2]{1,0:T(2,128)S(1)} collective-permute-done((s32[2,2]{1,0:T(2,128)S(1)}, s32[2,2]{1,0:T(2,128)S(1)}, u32[]{:S(2)}, u32[]{:S(2)}) %collective-permute-start.5) | collective-permute-done | bytes 48 | tf_op jit(solution)/shard_map/ppermute | solution.py:358
  30.1 0.0 collective-permute-start.7
  30.1 1.7 %shard_map.69 = (bf16[2,224,512]{2,1,0:T(8,128)(2,1)S(1)}, bf16[2,224,512]{2,1,0:T(8,128)(2,1)S(1)}) custom-call(s32[2,2]{1,0:T(2,128)S(1)} %collective-permute-done.5.ids_ref, bf16[4,2,256,512]{3,2,1,0:T(8,128)(2,1)} %bitcast.14), custom_call_target="tpu_custom_call" | custom-call | bytes 2000000 | tf_op jit(solution)/shard_map/pallas_call | solution.py:117
  31.8 0.0 copy-start.2
  31.8 0.0 copy-start
  31.8 0.0 copy-start.1
  31.8 1.9 %collective-permute-done.7.ids_ref = s32[2,2]{1,0:T(2,128)S(1)} collective-permute-done((s32[2,2]{1,0:T(2,128)S(1)}, s32[2,2]{1,0:T(2,128)S(1)}, u32[]{:S(2)}, u32[]{:S(2)}) %collective-permute-start.7) | collective-permute-done | bytes 48 | tf_op jit(solution)/shard_map/ppermute | solution.py:358
  33.7 0.1 collective-permute-start.10
  33.8 1.7 %shard_map.70 = (bf16[2,224,512]{2,1,0:T(8,128)(2,1)S(1)}, bf16[2,224,512]{2,1,0:T(8,128)(2,1)S(1)}) custom-call(s32[2,2]{1,0:T(2,128)S(1)} %collective-permute-done.7.ids_ref, bf16[4,2,256,512]{3,2,1,0:T(8,128)(2,1)} %bitcast.15), custom_call_target="tpu_custom_call" | custom-call | bytes 2000000 | tf_op jit(solution)/shard_map/pallas_call | solution.py:117
  35.5 0.0 collective-permute-done.2.e3_ref
  35.5 1.4 %collective-permute-start.11 = (bf16[2,224,512]{2,1,0:T(8,128)(2,1)S(1)}, bf16[2,224,512]{2,1,0:T(8,128)(2,1)S(1)}, u32[]{:S(2)}, u32[]{:S(2)}) collective-permute-start(bf16[2,224,512]{2,1,0:T(8,128)(2,1)S(1)} %get-tuple-element.26), channel_id=1, source_target_pairs={{0,3},{1,2},{2,1},{3,0},{4,7},{5,6},{6,5},{7,4},{8,11},{9,10},{10,... | collective-permute-start | bytes 1376264 | tf_op jit(solution)/shard_map/ppermute | solution.py:365
  36.9 0.0 collective-permute-done.1.e2_ref
  36.9 1.3 collective-permute-start.4
  38.2 0.0 collective-permute-done.e1_ref
  38.2 1.3 collective-permute-start.6
  39.5 0.0 collective-permute-done.9.r1_ref
  39.5 1.3 collective-permute-start.8
  40.8 0.0 copy-done.2
  40.8 0.0 copy-done
  40.8 0.0 copy-done.1
  40.8 1.9 %prepare.1 = (bf16[2,2,256,256]{3,2,1,0:T(8,128)(2,1)S(1)}, f32[256,128]{1,0:T(8,128)S(1)}) custom-call(s32[4,2,256]{2,1,0:T(2,128)S(1)} %bitcast.10, f32[4,2,256]{2,1,0:T(2,128)S(1)} %bitcast.11, f32[2,12,256]{2,1,0:T(8,128)S(1)} %copy.9.coef_ref), custom_call_target="tpu_custom_call" | custom-call | flops 4000000 | bytes 1000000 | tf_op jit(solution)/shard_map/prepare/pallas_call | solution.py:60
  42.7 0.4 collective-permute-done.10.r2_ref
  43.1 17.9 %collective-permute-done.11.r3_ref = bf16[2,224,512]{2,1,0:T(8,128)(2,1)S(1)} collective-permute-done((bf16[2,224,512]{2,1,0:T(8,128)(2,1)S(1)}, bf16[2,224,512]{2,1,0:T(8,128)(2,1)S(1)}, u32[]{:S(2)}, u32[]{:S(2)}) %collective-permute-start.11) | collective-permute-done | bytes 458784 | tf_op jit(solution)/shard_map/ppermute | solution.py:365
  61.1 3.4 %shard_map.71 = (bf16[2,3,256,512]{3,2,1,0:T(8,128)(2,1)}, f32[2,5,128,128]{3,2,1,0:T(8,128)S(1)}) custom-call(s32[2,2]{1,0:T(2,128)S(1)} %get-tuple-element.17.ids_ref, bf16[4,2,256,512]{3,2,1,0:T(8,128)(2,1)} %bitcast.16, bf16[4,2,32,512]{3,2,1,0:T(8,128)(2,1)S(1)} %collective-permute-done.e1_ref, ...), custom_call_target="tpu_custom_call" | custom-call | flops 700000000 | bytes 4000000 | tf_op jit(solution)/shard_map/pallas_call | solution.py:210
  64.4 0.0 collective-permute-done.4.r1_ref
  64.5 0.0 collective-permute-done.6.r2_ref
  64.5 12.2 %collective-permute-done.8.r3_ref = bf16[2,224,512]{2,1,0:T(8,128)(2,1)S(1)} collective-permute-done((bf16[2,224,512]{2,1,0:T(8,128)(2,1)S(1)}, bf16[2,224,512]{2,1,0:T(8,128)(2,1)S(1)}, u32[]{:S(2)}, u32[]{:S(2)}) %collective-permute-start.8) | collective-permute-done | bytes 458784 | tf_op jit(solution)/shard_map/ppermute | solution.py:365
  76.7 4.2 %shard_map.72 = (bf16[2,3,256,512]{3,2,1,0:T(8,128)(2,1)}, f32[5,128,128]{2,1,0:T(8,128)S(1)}, f32[5,128,128]{2,1,0:T(8,128)S(1)}) custom-call(s32[2,2]{1,0:T(2,128)S(1)} %get-tuple-element.17.ids_ref, bf16[4,2,256,512]{3,2,1,0:T(8,128)(2,1)} %bitcast.17, bf16[4,2,32,512]{3,2,1,0:T(8,128)(2,1)S(1)} %collective-permute-done.e1_ref, ...), custom_call_target="tpu_custom_call", output_to_operand_aliasing={{0}: (11, {})} | custom-call | flops 700000000 | bytes 4000000 | tf_op jit(solution)/shard_map/pallas_call | solution.py:210
  80.9 1.6 %collective-permute-start.12 = (f32[5,128,128]{2,1,0:T(8,128)S(1)}, f32[5,128,128]{2,1,0:T(8,128)S(1)}, u32[]{:S(2)}, u32[]{:S(2)}) collective-permute-start(f32[5,128,128]{2,1,0:T(8,128)S(1)} %get-tuple-element.31), channel_id=1, source_target_pairs={{0,4},{4,0},{1,5},{5,1},{2,6},{6,2},{3,7},{7,3},{8,12},{12,8},{9,1... | collective-permute-start | bytes 983048 | tf_op jit(solution)/shard_map/ppermute | solution.py:336
  82.4 1.3 collective-permute-done.12
  83.7 15.1 %all_to_all.10 = f32[16,40,128]{2,1,0:T(8,128)S(1)} all-to-all(f32[16,40,128]{2,1,0:T(8,128)S(1)} %bitcast.19), channel_id=1, replica_groups=mesh['y'=4,'z'=4,'core'=2,'x'=4] {'y','z'}, dimensions={0} | all-to-all | bytes 655360 | tf_op jit(solution)/shard_map/all_to_all | solution.py:337
  98.8 0.1 collective-permute-start.13
  98.9 2.6 %collective-permute-done.13 = f32[40,128]{1,0:T(8,128)S(1)} collective-permute-done((f32[40,128]{1,0:T(8,128)S(1)}, f32[40,128]{1,0:T(8,128)S(1)}, u32[]{:S(2)}, u32[]{:S(2)}) %collective-permute-start.13) | collective-permute-done | bytes 20512 | tf_op jit(solution)/shard_map/ppermute | solution.py:340
  101.5 1.6 %collective-permute-start.14 = (f32[40,128]{1,0:T(8,128)S(1)}, f32[40,128]{1,0:T(8,128)S(1)}, u32[]{:S(2)}, u32[]{:S(2)}) collective-permute-start(f32[40,128]{1,0:T(8,128)S(1)} %add.10), channel_id=1, source_target_pairs={{0,2},{1,3},{2,0},{3,1},{4,6},{5,7},{6,4},{7,5},{8,10},{9,11},{10,... | collective-permute-start | bytes 61448 | tf_op jit(solution)/shard_map/ppermute | solution.py:340
  103.2 2.6 %collective-permute-done.14 = f32[40,128]{1,0:T(8,128)S(1)} collective-permute-done((f32[40,128]{1,0:T(8,128)S(1)}, f32[40,128]{1,0:T(8,128)S(1)}, u32[]{:S(2)}, u32[]{:S(2)}) %collective-permute-start.14) | collective-permute-done | bytes 20512 | tf_op jit(solution)/shard_map/ppermute | solution.py:340
  105.8 11.4 %all_to_all.11 = f32[16,40,128]{2,1,0:T(8,128)S(1)} all-to-all(f32[16,40,128]{2,1,0:T(8,128)S(1)} %broadcast_in_dim.3), channel_id=1, replica_groups=mesh['y'=4,'z'=4,'core'=2,'x'=4] {'y','z'}, dimensions={0} | all-to-all | bytes 655360 | tf_op jit(solution)/shard_map/all_to_all | solution.py:341
  117.2 5.2 %collective-permute-start.15 = (f32[5,128,128]{2,1,0:T(8,128)S(1)}, f32[5,128,128]{2,1,0:T(8,128)S(1)}, u32[]{:S(2)}, u32[]{:S(2)}) collective-permute-start(f32[5,128,128]{2,1,0:T(8,128)S(1)} %bitcast.8), channel_id=1, source_target_pairs={{0,4},{4,0},{1,5},{5,1},{2,6},{6,2},{3,7},{7,3},{8,12},{12,8},{9,1... | collective-permute-start | bytes 983048 | tf_op jit(solution)/shard_map/ppermute | solution.py:342
  122.5 1.3 collective-permute-done.15.other_ref
  123.7 16.4 %factor.1 = f32[512,512]{1,0:T(8,128)} custom-call(f32[5,128,128]{2,1,0:T(8,128)S(1)} %bitcast.9, f32[5,128,128]{2,1,0:T(8,128)S(1)} %collective-permute-done.15.other_ref), custom_call_target="tpu_custom_call" | custom-call | tf_op jit(solution)/shard_map/factor/pallas_call | solution.py:320
  (7 shorter events, 0.1 us)
Async XLA Ops:
  1.6 3.1 %collective-permute-start.3 = (s32[2,2]{1,0:T(2,128)S(1)}, s32[2,2]{1,0:T(2,128)S(1)}, u32[]{:S(2)}, u32[]{:S(2)}) collective-permute-start(s32[2,2]{1,0:T(2,128)S(1)} %get-tuple-element.17.ids_ref), channel_id=1, source_target_pairs={{0,1},{1,0},{2,3},{3,2},{4,5},{5,4},{6,7},{7,6},{8,9},{9,8},{10,11... | collective-permute-start | bytes 56 | tf_op jit(solution)/shard_map/ppermute | solution.py:358
  6.4 33.0 %collective-permute-start.9 = (bf16[2,224,512]{2,1,0:T(8,128)(2,1)S(1)}, bf16[2,224,512]{2,1,0:T(8,128)(2,1)S(1)}, u32[]{:S(2)}, u32[]{:S(2)}) collective-permute-start(bf16[2,224,512]{2,1,0:T(8,128)(2,1)S(1)} %get-tuple-element.24), channel_id=1, source_target_pairs={{0,1},{1,0},{2,3},{3,2},{4,5},{5,4},{6,7},{7,6},{8,9},{9,8},{10,11... | collective-permute-start | bytes 1376264 | tf_op jit(solution)/shard_map/ppermute | solution.py:365
  8.0 27.5 %collective-permute-start.2 = (bf16[4,2,32,512]{3,2,1,0:T(8,128)(2,1)S(1)}, bf16[4,2,32,512]{3,2,1,0:T(8,128)(2,1)S(1)}, u32[]{:S(2)}, u32[]{:S(2)}) collective-permute-start(bf16[4,2,32,512]{3,2,1,0:T(8,128)(2,1)S(1)} %get-tuple-element.18), channel_id=1, source_target_pairs={{0,3},{1,2},{2,1},{3,0},{4,7},{5,6},{6,5},{7,4},{8,11},{9,10},{10,... | collective-permute-start | bytes 786440 | tf_op jit(solution)/shard_map/ppermute | solution.py:360
  9.8 27.1 %collective-permute-start.1 = (bf16[4,2,32,512]{3,2,1,0:T(8,128)(2,1)S(1)}, bf16[4,2,32,512]{3,2,1,0:T(8,128)(2,1)S(1)}, u32[]{:S(2)}, u32[]{:S(2)}) collective-permute-start(bf16[4,2,32,512]{3,2,1,0:T(8,128)(2,1)S(1)} %get-tuple-element.18), channel_id=1, source_target_pairs={{0,2},{1,3},{2,0},{3,1},{4,6},{5,7},{6,4},{7,5},{8,10},{9,11},{10,... | collective-permute-start | bytes 786440 | tf_op jit(solution)/shard_map/ppermute | solution.py:360
  10.4 27.8 %collective-permute-start = (bf16[4,2,32,512]{3,2,1,0:T(8,128)(2,1)S(1)}, bf16[4,2,32,512]{3,2,1,0:T(8,128)(2,1)S(1)}, u32[]{:S(2)}, u32[]{:S(2)}) collective-permute-start(bf16[4,2,32,512]{3,2,1,0:T(8,128)(2,1)S(1)} %get-tuple-element.18), channel_id=1, source_target_pairs={{0,1},{1,0},{2,3},{3,2},{4,5},{5,4},{6,7},{7,6},{8,9},{9,8},{10,11... | collective-permute-start | bytes 786440 | tf_op jit(solution)/shard_map/ppermute | solution.py:360
  11.2 18.8 %collective-permute-start.5 = (s32[2,2]{1,0:T(2,128)S(1)}, s32[2,2]{1,0:T(2,128)S(1)}, u32[]{:S(2)}, u32[]{:S(2)}) collective-permute-start(s32[2,2]{1,0:T(2,128)S(1)} %get-tuple-element.17.ids_ref), channel_id=1, source_target_pairs={{0,2},{1,3},{2,0},{3,1},{4,6},{5,7},{6,4},{7,5},{8,10},{9,11},{10,... | collective-permute-start | bytes 56 | tf_op jit(solution)/shard_map/ppermute | solution.py:358
  30.1 3.6 %collective-permute-start.7 = (s32[2,2]{1,0:T(2,128)S(1)}, s32[2,2]{1,0:T(2,128)S(1)}, u32[]{:S(2)}, u32[]{:S(2)}) collective-permute-start(s32[2,2]{1,0:T(2,128)S(1)} %get-tuple-element.17.ids_ref), channel_id=1, source_target_pairs={{0,3},{1,2},{2,1},{3,0},{4,7},{5,6},{6,5},{7,4},{8,11},{9,10},{10,... | collective-permute-start | bytes 56 | tf_op jit(solution)/shard_map/ppermute | solution.py:358
  31.8 9.0 %copy-start.2 = (f32[1,1,2,3,4,256]{5,4,3,2,1,0:T(4,128)S(1)}, f32[1,1,2,3,4,256]{5,4,3,2,1,0:T(4,128)}, u32[]{:S(2)}) copy-start(f32[1,1,2,3,4,256]{5,4,3,2,1,0:T(4,128)} %param.9) | copy-start | bytes 73732
  31.8 9.0 %copy-start = (s32[1,1,2,2,2,256]{5,4,3,2,1,0:T(2,128)S(1)}, s32[1,1,2,2,2,256]{5,4,3,2,1,0:T(2,128)}, u32[]{:S(2)}) copy-start(s32[1,1,2,2,2,256]{5,4,3,2,1,0:T(2,128)} %param.7) | copy-start | bytes 24580
  31.8 9.0 %copy-start.1 = (f32[1,1,2,2,2,256]{5,4,3,2,1,0:T(2,128)S(1)}, f32[1,1,2,2,2,256]{5,4,3,2,1,0:T(2,128)}, u32[]{:S(2)}) copy-start(f32[1,1,2,2,2,256]{5,4,3,2,1,0:T(2,128)} %param.8) | copy-start | bytes 24580
  33.7 9.4 %collective-permute-start.10 = (bf16[2,224,512]{2,1,0:T(8,128)(2,1)S(1)}, bf16[2,224,512]{2,1,0:T(8,128)(2,1)S(1)}, u32[]{:S(2)}, u32[]{:S(2)}) collective-permute-start(bf16[2,224,512]{2,1,0:T(8,128)(2,1)S(1)} %get-tuple-element.25), channel_id=1, source_target_pairs={{0,2},{1,3},{2,0},{3,1},{4,6},{5,7},{6,4},{7,5},{8,10},{9,11},{10,... | collective-permute-start | bytes 1376264 | tf_op jit(solution)/shard_map/ppermute | solution.py:365
  35.5 25.6 %collective-permute-start.11 = (bf16[2,224,512]{2,1,0:T(8,128)(2,1)S(1)}, bf16[2,224,512]{2,1,0:T(8,128)(2,1)S(1)}, u32[]{:S(2)}, u32[]{:S(2)}) collective-permute-start(bf16[2,224,512]{2,1,0:T(8,128)(2,1)S(1)} %get-tuple-element.26), channel_id=1, source_target_pairs={{0,3},{1,2},{2,1},{3,0},{4,7},{5,6},{6,5},{7,4},{8,11},{9,10},{10,... | collective-permute-start | bytes 1376264 | tf_op jit(solution)/shard_map/ppermute | solution.py:365
  36.9 27.5 %collective-permute-start.4 = (bf16[2,224,512]{2,1,0:T(8,128)(2,1)S(1)}, bf16[2,224,512]{2,1,0:T(8,128)(2,1)S(1)}, u32[]{:S(2)}, u32[]{:S(2)}) collective-permute-start(bf16[2,224,512]{2,1,0:T(8,128)(2,1)S(1)} %get-tuple-element.19), channel_id=1, source_target_pairs={{0,1},{1,0},{2,3},{3,2},{4,5},{5,4},{6,7},{7,6},{8,9},{9,8},{10,11... | collective-permute-start | bytes 1376264 | tf_op jit(solution)/shard_map/ppermute | solution.py:365
  38.2 26.3 %collective-permute-start.6 = (bf16[2,224,512]{2,1,0:T(8,128)(2,1)S(1)}, bf16[2,224,512]{2,1,0:T(8,128)(2,1)S(1)}, u32[]{:S(2)}, u32[]{:S(2)}) collective-permute-start(bf16[2,224,512]{2,1,0:T(8,128)(2,1)S(1)} %get-tuple-element.20), channel_id=1, source_target_pairs={{0,2},{1,3},{2,0},{3,1},{4,6},{5,7},{6,4},{7,5},{8,10},{9,11},{10,... | collective-permute-start | bytes 1376264 | tf_op jit(solution)/shard_map/ppermute | solution.py:365
  39.5 37.2 %collective-permute-start.8 = (bf16[2,224,512]{2,1,0:T(8,128)(2,1)S(1)}, bf16[2,224,512]{2,1,0:T(8,128)(2,1)S(1)}, u32[]{:S(2)}, u32[]{:S(2)}) collective-permute-start(bf16[2,224,512]{2,1,0:T(8,128)(2,1)S(1)} %get-tuple-element.21), channel_id=1, source_target_pairs={{0,3},{1,2},{2,1},{3,0},{4,7},{5,6},{6,5},{7,4},{8,11},{9,10},{10,... | collective-permute-start | bytes 1376264 | tf_op jit(solution)/shard_map/ppermute | solution.py:365
  80.9 2.8 %collective-permute-start.12 = (f32[5,128,128]{2,1,0:T(8,128)S(1)}, f32[5,128,128]{2,1,0:T(8,128)S(1)}, u32[]{:S(2)}, u32[]{:S(2)}) collective-permute-start(f32[5,128,128]{2,1,0:T(8,128)S(1)} %get-tuple-element.31), channel_id=1, source_target_pairs={{0,4},{4,0},{1,5},{5,1},{2,6},{6,2},{3,7},{7,3},{8,12},{12,8},{9,1... | collective-permute-start | bytes 983048 | tf_op jit(solution)/shard_map/ppermute | solution.py:336
  98.8 2.7 %collective-permute-start.13 = (f32[40,128]{1,0:T(8,128)S(1)}, f32[40,128]{1,0:T(8,128)S(1)}, u32[]{:S(2)}, u32[]{:S(2)}) collective-permute-start(f32[40,128]{1,0:T(8,128)S(1)} %reduce_sum.9), channel_id=1, source_target_pairs={{0,1},{1,0},{2,3},{3,2},{4,5},{5,4},{6,7},{7,6},{8,9},{9,8},{10,11... | collective-permute-start | bytes 61448 | tf_op jit(solution)/shard_map/ppermute | solution.py:340
  101.5 4.3 %collective-permute-start.14 = (f32[40,128]{1,0:T(8,128)S(1)}, f32[40,128]{1,0:T(8,128)S(1)}, u32[]{:S(2)}, u32[]{:S(2)}) collective-permute-start(f32[40,128]{1,0:T(8,128)S(1)} %add.10), channel_id=1, source_target_pairs={{0,2},{1,3},{2,0},{3,1},{4,6},{5,7},{6,4},{7,5},{8,10},{9,11},{10,... | collective-permute-start | bytes 61448 | tf_op jit(solution)/shard_map/ppermute | solution.py:340
  117.2 6.5 %collective-permute-start.15 = (f32[5,128,128]{2,1,0:T(8,128)S(1)}, f32[5,128,128]{2,1,0:T(8,128)S(1)}, u32[]{:S(2)}, u32[]{:S(2)}) collective-permute-start(f32[5,128,128]{2,1,0:T(8,128)S(1)} %bitcast.8), channel_id=1, source_target_pairs={{0,4},{4,0},{1,5},{5,1},{2,6},{6,2},{3,7},{7,3},{8,12},{12,8},{9,1... | collective-permute-start | bytes 983048 | tf_op jit(solution)/shard_map/ppermute | solution.py:342

commit v2 on v1

--- a/solution.py
+++ b/solution.py
@@ -127,10 +127,10 @@
 
 def world_kernel(w, ids_ref, cam_ref, e1_ref, e2_ref, e3_ref, r1_ref, r2_ref, r3_ref, mats_ref, coef_ref, *rest):
     if w:
-        gin_ref, _, vel_ref, mine_ref, other_ref, tiles, interp, sem = rest
+        gin_ref, _, vel_out, mine_ref, other_ref, tiles, interp, vel_ref, sem, out_sem = rest
     else:
-        vel_ref, gram_ref, tiles, interp, sem = rest
-    cells, snaps = vel_ref.shape[2], vel_ref.shape[3]
+        vel_out, gram_ref, tiles, interp, vel_ref, sem, out_sem = rest
+    _, cells, snaps = vel_ref.shape
     firsts, others = (None, e1_ref, e2_ref, e3_ref), (None, r1_ref, r2_ref, r3_ref)
     indices, dists = [], []
     for c in range(2):
@@ -167,11 +167,13 @@
             total = coef_ref[q, at : at + 1] * parts[0]
             for i in range(1, 4):
                 total = total + coef_ref[q, at + i : at + i + 1] * parts[i]
-            vel_ref[0, k, q, :] = total.astype(BF16)
+            vel_ref[k, q, :] = total.astype(BF16)
         return 0
 
     lax.fori_loop(0, cells // rows, cell_rows, 0)
-    flat = vel_ref[0].reshape(3 * cells, snaps)
+    leave = pltpu.make_async_copy(vel_ref, vel_out.at[w], out_sem)
+    leave.start()
+    flat = vel_ref[...].reshape(3 * cells, snaps)
     core = lax.axis_index("core")
     for i in range(snaps // 256):
         left = flat[:, 256 * i : 256 * (i + 1)]
@@ -185,14 +187,14 @@
                     gram_ref[half, at] = part
                 else:
                     parts.append((half, at, part + gin_ref[half, at]))
-        if w == 0:
-            continue
-        for side in range(2):
+        for side in range(2 if w else 0):
 
             @pl.when(core == side)
             def _():
                 for half, at, part in parts:
                     (mine_ref if half == side else other_ref)[at] = part
+
+    leave.wait()
 
 
 def world(w, ids, cam, firsts, recv, mats, coef, carry):
@@ -209,11 +211,10 @@
         aliases = {len(args) - 1: 0}
     return pl.pallas_call(
         functools.partial(world_kernel, w),
-        grid=(1,),
         in_specs=in_specs,
         out_specs=(
-            pl.BlockSpec((1, 3, cells, snaps), lambda _: (w, 0, 0, 0)),
-            *[pl.BlockSpec(grams, lambda _: (0,) * len(grams))] * outs,
+            ANY,
+            *[VM] * outs,
         ),
         out_shape=(
             jax.ShapeDtypeStruct((world_tiles, 3, cells, snaps), BF16),
@@ -222,7 +223,9 @@
         scratch_shapes=[
             pltpu.VMEM((2, 2, cam.shape[2], snaps), BF16),
             pltpu.VMEM((4, cells, snaps), F32),
+            pltpu.VMEM((3, cells, snaps), BF16),
             pltpu.SemaphoreType.DMA((2,)),
+            pltpu.SemaphoreType.DMA,
         ],
         input_output_aliases=aliases,
         compiler_params=pltpu.CompilerParams(vmem_limit_bytes=16 << 20),
@@ -277,7 +280,7 @@
     return lax.dot_general(a, b, ((dims[:1], dims[1:]), ((), ())), precision=lax.Precision.HIGHEST, preferred_element_type=F32)
 
 
-def factor_kernel(own_ref, other_ref, o_ref, s_ref):
+def factor_kernel(own_ref, other_ref, out_ref, s_ref, o_ref, sem):
     n, size = o_ref.shape[0], 128
     parts = n // size
     core = lax.axis_index("core")
@@ -290,6 +293,10 @@
                     s_ref[row * size : (row + 1) * size, column * size : (column + 1) * size] = ref[at]
 
     o_ref[...] = jnp.zeros_like(o_ref)
+
+    def leave(q):
+        rows = pl.ds(q * size, size)
+        return pltpu.make_async_copy(o_ref.at[rows], out_ref.at[rows], sem.at[q])
 
     def panel(p, _):
         off = pl.multiple_of(p * size, size)
@@ -305,6 +312,7 @@
                 col = lax.broadcasted_iota(jnp.int32, (size, wide), 1)
                 r = jnp.where(col >= row, r, 0.0)
                 o_ref[lo : lo + size, lo:] = r
+                leave(q).start()
                 if q < parts - 1:
                     for m in range(q + 1, parts):
                         at = m * size
@@ -314,6 +322,8 @@
         return 0
 
     lax.fori_loop(0, parts, panel, 0)
+    for q in range(parts):
+        leave(q).wait()
 
 
 def factor(own, other, n):
@@ -321,8 +331,8 @@
         factor_kernel,
         out_shape=jax.ShapeDtypeStruct((n, n), F32),
         in_specs=[VM, VM],
-        out_specs=VM,
-        scratch_shapes=[pltpu.VMEM((n, n), F32)],
+        out_specs=ANY,
+        scratch_shapes=[pltpu.VMEM((n, n), F32), pltpu.VMEM((n, n), F32), pltpu.SemaphoreType.DMA((n // 128,))],
         compiler_params=pltpu.CompilerParams(vmem_limit_bytes=16 << 20),
         name="factor",
     )(own, other)

time: 140 us -> 140 us (level)
  no operation moved by 1% of the time
where the time goes in v2:
time: 140 us; the launch traced here: 139 us
  waiting for transfers between devices  57.5 us (41%)
  Pallas kernels  30.9 us (22%)
  blocking collectives  26.5 us (19%)
  starting transfers between devices  23.2 us (17%)
    ppermute x6, waiting for transfers between devices, program(): received[w][k] = lax.ppermute(payload[w], 'x', swaps[k])  30.6 us
    ppermute x3, waiting for transfers between devices, program(): asked.append(lax.ppermute(ids, 'x', swaps[k]))  19.2 us
    pallas_call x1, Pallas kernels, factor(): pl.pallas_call(factor_kernel, out_shape=jax.ShapeDtypeStruct((n, n), F32)...  16.1 us
    all_to_all x1, blocking collectives, sum_devices(): pieces = lax.all_to_all(mine.reshape(planes, -1, 128), PLANE, 0, 0)  15.1 us
    all_to_all x1, blocking collectives, sum_devices(): lax.all_to_all(jnp.broadcast_to(piece * scale, pieces.shape), PLANE, 0, 0)  11.4 us
    ppermute x6, starting transfers between devices, program(): received[w][k] = lax.ppermute(payload[w], 'x', swaps[k])  6.87 us
    pallas_call x2, Pallas kernels, world(): pl.pallas_call(functools.partial(world_kernel, w), in_specs=in_specs, out...  6.75 us
    ppermute x2, waiting for transfers between devices, sum_devices(): lax.ppermute(piece, 'x', [(i, i ^ k) for i in range(groups)])  5.25 us
  transfers between devices with their start and end apart: 16, of which 10 were waited for; matrix products, arithmetic and copies ran while one was open for 0% of the time, Pallas kernels for 6%

profile of v2, /device:TPU:1, one launch (start us, length us, event | category | flops | bytes accessed | tf_op | source)
XLA Modules:
  0.0 139.2 jit_solution(3435873465796270126)
XLA Ops:
  0.6 1.0 early.1
  1.6 2.1 %collective-permute-start.3 = (s32[2,2]{1,0:T(2,128)S(1)}, s32[2,2]{1,0:T(2,128)S(1)}, u32[]{:S(2)}, u32[]{:S(2)}) collective-permute-start(s32[2,2]{1,0:T(2,128)S(1)} %get-tuple-element.17.ids_ref), channel_id=1, source_target_pairs={{0,1},{1,0},{2,3},{3,2},{4,5},{5,4},{6,7},{7,6},{8,9},{9,8},{10,11... | collective-permute-start | bytes 56 | tf_op jit(solution)/shard_map/ppermute | solution.py:368
  3.7 1.0 collective-permute-done.3.ids_ref
  4.7 1.7 %shard_map.68 = (bf16[2,224,512]{2,1,0:T(8,128)(2,1)S(1)}, bf16[2,224,512]{2,1,0:T(8,128)(2,1)S(1)}) custom-call(s32[2,2]{1,0:T(2,128)S(1)} %collective-permute-done.3.ids_ref, bf16[4,2,256,512]{3,2,1,0:T(8,128)(2,1)} %bitcast.13), custom_call_target="tpu_custom_call" | custom-call | bytes 2000000 | tf_op jit(solution)/shard_map/pallas_call | solution.py:117
  6.4 1.5 %collective-permute-start.9 = (bf16[2,224,512]{2,1,0:T(8,128)(2,1)S(1)}, bf16[2,224,512]{2,1,0:T(8,128)(2,1)S(1)}, u32[]{:S(2)}, u32[]{:S(2)}) collective-permute-start(bf16[2,224,512]{2,1,0:T(8,128)(2,1)S(1)} %get-tuple-element.24), channel_id=1, source_target_pairs={{0,1},{1,0},{2,3},{3,2},{4,5},{5,4},{6,7},{7,6},{8,9},{9,8},{10,11... | collective-permute-start | bytes 1376264 | tf_op jit(solution)/shard_map/ppermute | solution.py:375
  8.0 1.8 %collective-permute-start.2 = (bf16[4,2,32,512]{3,2,1,0:T(8,128)(2,1)S(1)}, bf16[4,2,32,512]{3,2,1,0:T(8,128)(2,1)S(1)}, u32[]{:S(2)}, u32[]{:S(2)}) collective-permute-start(bf16[4,2,32,512]{3,2,1,0:T(8,128)(2,1)S(1)} %get-tuple-element.18), channel_id=1, source_target_pairs={{0,3},{1,2},{2,1},{3,0},{4,7},{5,6},{6,5},{7,4},{8,11},{9,10},{10,... | collective-permute-start | bytes 786440 | tf_op jit(solution)/shard_map/ppermute | solution.py:370
  9.8 0.6 collective-permute-start.1
  10.4 0.8 collective-permute-start
  11.2 2.5 %collective-permute-start.5 = (s32[2,2]{1,0:T(2,128)S(1)}, s32[2,2]{1,0:T(2,128)S(1)}, u32[]{:S(2)}, u32[]{:S(2)}) collective-permute-start(s32[2,2]{1,0:T(2,128)S(1)} %get-tuple-element.17.ids_ref), channel_id=1, source_target_pairs={{0,2},{1,3},{2,0},{3,1},{4,6},{5,7},{6,4},{7,5},{8,10},{9,11},{10,... | collective-permute-start | bytes 56 | tf_op jit(solution)/shard_map/ppermute | solution.py:368
  13.7 16.4 %collective-permute-done.5.ids_ref = s32[2,2]{1,0:T(2,128)S(1)} collective-permute-done((s32[2,2]{1,0:T(2,128)S(1)}, s32[2,2]{1,0:T(2,128)S(1)}, u32[]{:S(2)}, u32[]{:S(2)}) %collective-permute-start.5) | collective-permute-done | bytes 48 | tf_op jit(solution)/shard_map/ppermute | solution.py:368
  30.1 0.0 collective-permute-start.7
  30.1 1.7 %shard_map.69 = (bf16[2,224,512]{2,1,0:T(8,128)(2,1)S(1)}, bf16[2,224,512]{2,1,0:T(8,128)(2,1)S(1)}) custom-call(s32[2,2]{1,0:T(2,128)S(1)} %collective-permute-done.5.ids_ref, bf16[4,2,256,512]{3,2,1,0:T(8,128)(2,1)} %bitcast.14), custom_call_target="tpu_custom_call" | custom-call | bytes 2000000 | tf_op jit(solution)/shard_map/pallas_call | solution.py:117
  31.8 0.0 copy-start.2
  31.8 0.0 copy-start
  31.8 0.0 copy-start.1
  31.8 1.9 %collective-permute-done.7.ids_ref = s32[2,2]{1,0:T(2,128)S(1)} collective-permute-done((s32[2,2]{1,0:T(2,128)S(1)}, s32[2,2]{1,0:T(2,128)S(1)}, u32[]{:S(2)}, u32[]{:S(2)}) %collective-permute-start.7) | collective-permute-done | bytes 48 | tf_op jit(solution)/shard_map/ppermute | solution.py:368
  33.7 0.1 collective-permute-start.10
  33.8 1.7 %shard_map.70 = (bf16[2,224,512]{2,1,0:T(8,128)(2,1)S(1)}, bf16[2,224,512]{2,1,0:T(8,128)(2,1)S(1)}) custom-call(s32[2,2]{1,0:T(2,128)S(1)} %collective-permute-done.7.ids_ref, bf16[4,2,256,512]{3,2,1,0:T(8,128)(2,1)} %bitcast.15), custom_call_target="tpu_custom_call" | custom-call | bytes 2000000 | tf_op jit(solution)/shard_map/pallas_call | solution.py:117
  35.5 0.0 collective-permute-done.2.e3_ref
  35.5 1.4 %collective-permute-start.11 = (bf16[2,224,512]{2,1,0:T(8,128)(2,1)S(1)}, bf16[2,224,512]{2,1,0:T(8,128)(2,1)S(1)}, u32[]{:S(2)}, u32[]{:S(2)}) collective-permute-start(bf16[2,224,512]{2,1,0:T(8,128)(2,1)S(1)} %get-tuple-element.26), channel_id=1, source_target_pairs={{0,3},{1,2},{2,1},{3,0},{4,7},{5,6},{6,5},{7,4},{8,11},{9,10},{10,... | collective-permute-start | bytes 1376264 | tf_op jit(solution)/shard_map/ppermute | solution.py:375
  36.9 0.0 collective-permute-done.1.e2_ref
  36.9 1.3 collective-permute-start.4
  38.2 0.0 collective-permute-done.e1_ref
  38.2 1.3 collective-permute-start.6
  39.5 0.0 collective-permute-done.9.r1_ref
  39.5 1.3 collective-permute-start.8
  40.8 0.0 copy-done.2
  40.8 0.0 copy-done
  40.8 0.0 copy-done.1
  40.8 1.9 %prepare.1 = (bf16[2,2,256,256]{3,2,1,0:T(8,128)(2,1)S(1)}, f32[256,128]{1,0:T(8,128)S(1)}) custom-call(s32[4,2,256]{2,1,0:T(2,128)S(1)} %bitcast.10, f32[4,2,256]{2,1,0:T(2,128)S(1)} %bitcast.11, f32[2,12,256]{2,1,0:T(8,128)S(1)} %copy.9.coef_ref), custom_call_target="tpu_custom_call" | custom-call | flops 4000000 | bytes 1000000 | tf_op jit(solution)/shard_map/prepare/pallas_call | solution.py:60
  42.7 0.4 collective-permute-done.10.r2_ref
  43.1 17.9 %collective-permute-done.11.r3_ref = bf16[2,224,512]{2,1,0:T(8,128)(2,1)S(1)} collective-permute-done((bf16[2,224,512]{2,1,0:T(8,128)(2,1)S(1)}, bf16[2,224,512]{2,1,0:T(8,128)(2,1)S(1)}, u32[]{:S(2)}, u32[]{:S(2)}) %collective-permute-start.11) | collective-permute-done | bytes 458784 | tf_op jit(solution)/shard_map/ppermute | solution.py:375
  61.1 3.4 %shard_map.71 = (bf16[2,3,256,512]{3,2,1,0:T(8,128)(2,1)}, f32[2,5,128,128]{3,2,1,0:T(8,128)S(1)}) custom-call(s32[2,2]{1,0:T(2,128)S(1)} %get-tuple-element.17.ids_ref, bf16[4,2,256,512]{3,2,1,0:T(8,128)(2,1)} %bitcast.16, bf16[4,2,32,512]{3,2,1,0:T(8,128)(2,1)S(1)} %collective-permute-done.e1_ref, ...), custom_call_target="tpu_custom_call" | custom-call | flops 700000000 | bytes 4000000 | tf_op jit(solution)/shard_map/pallas_call | solution.py:212
  64.5 0.0 collective-permute-done.4.r1_ref
  64.5 0.0 collective-permute-done.6.r2_ref
  64.5 12.2 %collective-permute-done.8.r3_ref = bf16[2,224,512]{2,1,0:T(8,128)(2,1)S(1)} collective-permute-done((bf16[2,224,512]{2,1,0:T(8,128)(2,1)S(1)}, bf16[2,224,512]{2,1,0:T(8,128)(2,1)S(1)}, u32[]{:S(2)}, u32[]{:S(2)}) %collective-permute-start.8) | collective-permute-done | bytes 458784 | tf_op jit(solution)/shard_map/ppermute | solution.py:375
  76.7 3.4 %shard_map.72 = (bf16[2,3,256,512]{3,2,1,0:T(8,128)(2,1)}, f32[5,128,128]{2,1,0:T(8,128)S(1)}, f32[5,128,128]{2,1,0:T(8,128)S(1)}) custom-call(s32[2,2]{1,0:T(2,128)S(1)} %get-tuple-element.17.ids_ref, bf16[4,2,256,512]{3,2,1,0:T(8,128)(2,1)} %bitcast.17, bf16[4,2,32,512]{3,2,1,0:T(8,128)(2,1)S(1)} %collective-permute-done.e1_ref, ...), custom_call_target="tpu_custom_call", output_to_operand_aliasing={{0}: (11, {})} | custom-call | flops 700000000 | bytes 4000000 | tf_op jit(solution)/shard_map/pallas_call | solution.py:212
  80.1 1.6 %collective-permute-start.12 = (f32[5,128,128]{2,1,0:T(8,128)S(1)}, f32[5,128,128]{2,1,0:T(8,128)S(1)}, u32[]{:S(2)}, u32[]{:S(2)}) collective-permute-start(f32[5,128,128]{2,1,0:T(8,128)S(1)} %get-tuple-element.31), channel_id=1, source_target_pairs={{0,4},{4,0},{1,5},{5,1},{2,6},{6,2},{3,7},{7,3},{8,12},{12,8},{9,1... | collective-permute-start | bytes 983048 | tf_op jit(solution)/shard_map/ppermute | solution.py:346
  81.7 1.3 collective-permute-done.12
  83.0 15.1 %all_to_all.10 = f32[16,40,128]{2,1,0:T(8,128)S(1)} all-to-all(f32[16,40,128]{2,1,0:T(8,128)S(1)} %bitcast.19), channel_id=1, replica_groups=mesh['y'=4,'z'=4,'core'=2,'x'=4] {'y','z'}, dimensions={0} | all-to-all | bytes 655360 | tf_op jit(solution)/shard_map/all_to_all | solution.py:347
  98.1 0.1 collective-permute-start.13
  98.1 2.6 %collective-permute-done.13 = f32[40,128]{1,0:T(8,128)S(1)} collective-permute-done((f32[40,128]{1,0:T(8,128)S(1)}, f32[40,128]{1,0:T(8,128)S(1)}, u32[]{:S(2)}, u32[]{:S(2)}) %collective-permute-start.13) | collective-permute-done | bytes 20512 | tf_op jit(solution)/shard_map/ppermute | solution.py:350
  100.8 1.6 %collective-permute-start.14 = (f32[40,128]{1,0:T(8,128)S(1)}, f32[40,128]{1,0:T(8,128)S(1)}, u32[]{:S(2)}, u32[]{:S(2)}) collective-permute-start(f32[40,128]{1,0:T(8,128)S(1)} %add.10), channel_id=1, source_target_pairs={{0,2},{1,3},{2,0},{3,1},{4,6},{5,7},{6,4},{7,5},{8,10},{9,11},{10,... | collective-permute-start | bytes 61448 | tf_op jit(solution)/shard_map/ppermute | solution.py:350
  102.4 2.6 %collective-permute-done.14 = f32[40,128]{1,0:T(8,128)S(1)} collective-permute-done((f32[40,128]{1,0:T(8,128)S(1)}, f32[40,128]{1,0:T(8,128)S(1)}, u32[]{:S(2)}, u32[]{:S(2)}) %collective-permute-start.14) | collective-permute-done | bytes 20512 | tf_op jit(solution)/shard_map/ppermute | solution.py:350
  105.1 11.4 %all_to_all.11 = f32[16,40,128]{2,1,0:T(8,128)S(1)} all-to-all(f32[16,40,128]{2,1,0:T(8,128)S(1)} %broadcast_in_dim.3), channel_id=1, replica_groups=mesh['y'=4,'z'=4,'core'=2,'x'=4] {'y','z'}, dimensions={0} | all-to-all | bytes 655360 | tf_op jit(solution)/shard_map/all_to_all | solution.py:351
  116.5 5.2 %collective-permute-start.15 = (f32[5,128,128]{2,1,0:T(8,128)S(1)}, f32[5,128,128]{2,1,0:T(8,128)S(1)}, u32[]{:S(2)}, u32[]{:S(2)}) collective-permute-start(f32[5,128,128]{2,1,0:T(8,128)S(1)} %bitcast.8), channel_id=1, source_target_pairs={{0,4},{4,0},{1,5},{5,1},{2,6},{6,2},{3,7},{7,3},{8,12},{12,8},{9,1... | collective-permute-start | bytes 983048 | tf_op jit(solution)/shard_map/ppermute | solution.py:352
  121.7 1.3 collective-permute-done.15.other_ref
  123.0 16.1 %factor.1 = f32[512,512]{1,0:T(8,128)} custom-call(f32[5,128,128]{2,1,0:T(8,128)S(1)} %bitcast.9, f32[5,128,128]{2,1,0:T(8,128)S(1)} %collective-permute-done.15.other_ref), custom_call_target="tpu_custom_call" | custom-call | tf_op jit(solution)/shard_map/factor/pallas_call | solution.py:330
  (7 shorter events, 0.1 us)
Async XLA Ops:
  1.6 3.1 %collective-permute-start.3 = (s32[2,2]{1,0:T(2,128)S(1)}, s32[2,2]{1,0:T(2,128)S(1)}, u32[]{:S(2)}, u32[]{:S(2)}) collective-permute-start(s32[2,2]{1,0:T(2,128)S(1)} %get-tuple-element.17.ids_ref), channel_id=1, source_target_pairs={{0,1},{1,0},{2,3},{3,2},{4,5},{5,4},{6,7},{7,6},{8,9},{9,8},{10,11... | collective-permute-start | bytes 56 | tf_op jit(solution)/shard_map/ppermute | solution.py:368
  6.4 33.0 %collective-permute-start.9 = (bf16[2,224,512]{2,1,0:T(8,128)(2,1)S(1)}, bf16[2,224,512]{2,1,0:T(8,128)(2,1)S(1)}, u32[]{:S(2)}, u32[]{:S(2)}) collective-permute-start(bf16[2,224,512]{2,1,0:T(8,128)(2,1)S(1)} %get-tuple-element.24), channel_id=1, source_target_pairs={{0,1},{1,0},{2,3},{3,2},{4,5},{5,4},{6,7},{7,6},{8,9},{9,8},{10,11... | collective-permute-start | bytes 1376264 | tf_op jit(solution)/shard_map/ppermute | solution.py:375
  8.0 27.5 %collective-permute-start.2 = (bf16[4,2,32,512]{3,2,1,0:T(8,128)(2,1)S(1)}, bf16[4,2,32,512]{3,2,1,0:T(8,128)(2,1)S(1)}, u32[]{:S(2)}, u32[]{:S(2)}) collective-permute-start(bf16[4,2,32,512]{3,2,1,0:T(8,128)(2,1)S(1)} %get-tuple-element.18), channel_id=1, source_target_pairs={{0,3},{1,2},{2,1},{3,0},{4,7},{5,6},{6,5},{7,4},{8,11},{9,10},{10,... | collective-permute-start | bytes 786440 | tf_op jit(solution)/shard_map/ppermute | solution.py:370
  9.8 27.1 %collective-permute-start.1 = (bf16[4,2,32,512]{3,2,1,0:T(8,128)(2,1)S(1)}, bf16[4,2,32,512]{3,2,1,0:T(8,128)(2,1)S(1)}, u32[]{:S(2)}, u32[]{:S(2)}) collective-permute-start(bf16[4,2,32,512]{3,2,1,0:T(8,128)(2,1)S(1)} %get-tuple-element.18), channel_id=1, source_target_pairs={{0,2},{1,3},{2,0},{3,1},{4,6},{5,7},{6,4},{7,5},{8,10},{9,11},{10,... | collective-permute-start | bytes 786440 | tf_op jit(solution)/shard_map/ppermute | solution.py:370
  10.4 27.8 %collective-permute-start = (bf16[4,2,32,512]{3,2,1,0:T(8,128)(2,1)S(1)}, bf16[4,2,32,512]{3,2,1,0:T(8,128)(2,1)S(1)}, u32[]{:S(2)}, u32[]{:S(2)}) collective-permute-start(bf16[4,2,32,512]{3,2,1,0:T(8,128)(2,1)S(1)} %get-tuple-element.18), channel_id=1, source_target_pairs={{0,1},{1,0},{2,3},{3,2},{4,5},{5,4},{6,7},{7,6},{8,9},{9,8},{10,11... | collective-permute-start | bytes 786440 | tf_op jit(solution)/shard_map/ppermute | solution.py:370
  11.2 18.8 %collective-permute-start.5 = (s32[2,2]{1,0:T(2,128)S(1)}, s32[2,2]{1,0:T(2,128)S(1)}, u32[]{:S(2)}, u32[]{:S(2)}) collective-permute-start(s32[2,2]{1,0:T(2,128)S(1)} %get-tuple-element.17.ids_ref), channel_id=1, source_target_pairs={{0,2},{1,3},{2,0},{3,1},{4,6},{5,7},{6,4},{7,5},{8,10},{9,11},{10,... | collective-permute-start | bytes 56 | tf_op jit(solution)/shard_map/ppermute | solution.py:368
  30.1 3.6 %collective-permute-start.7 = (s32[2,2]{1,0:T(2,128)S(1)}, s32[2,2]{1,0:T(2,128)S(1)}, u32[]{:S(2)}, u32[]{:S(2)}) collective-permute-start(s32[2,2]{1,0:T(2,128)S(1)} %get-tuple-element.17.ids_ref), channel_id=1, source_target_pairs={{0,3},{1,2},{2,1},{3,0},{4,7},{5,6},{6,5},{7,4},{8,11},{9,10},{10,... | collective-permute-start | bytes 56 | tf_op jit(solution)/shard_map/ppermute | solution.py:368
  31.8 9.0 %copy-start.2 = (f32[1,1,2,3,4,256]{5,4,3,2,1,0:T(4,128)S(1)}, f32[1,1,2,3,4,256]{5,4,3,2,1,0:T(4,128)}, u32[]{:S(2)}) copy-start(f32[1,1,2,3,4,256]{5,4,3,2,1,0:T(4,128)} %param.9) | copy-start | bytes 73732
  31.8 9.0 %copy-start = (s32[1,1,2,2,2,256]{5,4,3,2,1,0:T(2,128)S(1)}, s32[1,1,2,2,2,256]{5,4,3,2,1,0:T(2,128)}, u32[]{:S(2)}) copy-start(s32[1,1,2,2,2,256]{5,4,3,2,1,0:T(2,128)} %param.7) | copy-start | bytes 24580
  31.8 9.0 %copy-start.1 = (f32[1,1,2,2,2,256]{5,4,3,2,1,0:T(2,128)S(1)}, f32[1,1,2,2,2,256]{5,4,3,2,1,0:T(2,128)}, u32[]{:S(2)}) copy-start(f32[1,1,2,2,2,256]{5,4,3,2,1,0:T(2,128)} %param.8) | copy-start | bytes 24580
  33.7 9.4 %collective-permute-start.10 = (bf16[2,224,512]{2,1,0:T(8,128)(2,1)S(1)}, bf16[2,224,512]{2,1,0:T(8,128)(2,1)S(1)}, u32[]{:S(2)}, u32[]{:S(2)}) collective-permute-start(bf16[2,224,512]{2,1,0:T(8,128)(2,1)S(1)} %get-tuple-element.25), channel_id=1, source_target_pairs={{0,2},{1,3},{2,0},{3,1},{4,6},{5,7},{6,4},{7,5},{8,10},{9,11},{10,... | collective-permute-start | bytes 1376264 | tf_op jit(solution)/shard_map/ppermute | solution.py:375
  35.5 25.6 %collective-permute-start.11 = (bf16[2,224,512]{2,1,0:T(8,128)(2,1)S(1)}, bf16[2,224,512]{2,1,0:T(8,128)(2,1)S(1)}, u32[]{:S(2)}, u32[]{:S(2)}) collective-permute-start(bf16[2,224,512]{2,1,0:T(8,128)(2,1)S(1)} %get-tuple-element.26), channel_id=1, source_target_pairs={{0,3},{1,2},{2,1},{3,0},{4,7},{5,6},{6,5},{7,4},{8,11},{9,10},{10,... | collective-permute-start | bytes 1376264 | tf_op jit(solution)/shard_map/ppermute | solution.py:375
  36.9 27.5 %collective-permute-start.4 = (bf16[2,224,512]{2,1,0:T(8,128)(2,1)S(1)}, bf16[2,224,512]{2,1,0:T(8,128)(2,1)S(1)}, u32[]{:S(2)}, u32[]{:S(2)}) collective-permute-start(bf16[2,224,512]{2,1,0:T(8,128)(2,1)S(1)} %get-tuple-element.19), channel_id=1, source_target_pairs={{0,1},{1,0},{2,3},{3,2},{4,5},{5,4},{6,7},{7,6},{8,9},{9,8},{10,11... | collective-permute-start | bytes 1376264 | tf_op jit(solution)/shard_map/ppermute | solution.py:375
  38.2 26.3 %collective-permute-start.6 = (bf16[2,224,512]{2,1,0:T(8,128)(2,1)S(1)}, bf16[2,224,512]{2,1,0:T(8,128)(2,1)S(1)}, u32[]{:S(2)}, u32[]{:S(2)}) collective-permute-start(bf16[2,224,512]{2,1,0:T(8,128)(2,1)S(1)} %get-tuple-element.20), channel_id=1, source_target_pairs={{0,2},{1,3},{2,0},{3,1},{4,6},{5,7},{6,4},{7,5},{8,10},{9,11},{10,... | collective-permute-start | bytes 1376264 | tf_op jit(solution)/shard_map/ppermute | solution.py:375
  39.5 37.2 %collective-permute-start.8 = (bf16[2,224,512]{2,1,0:T(8,128)(2,1)S(1)}, bf16[2,224,512]{2,1,0:T(8,128)(2,1)S(1)}, u32[]{:S(2)}, u32[]{:S(2)}) collective-permute-start(bf16[2,224,512]{2,1,0:T(8,128)(2,1)S(1)} %get-tuple-element.21), channel_id=1, source_target_pairs={{0,3},{1,2},{2,1},{3,0},{4,7},{5,6},{6,5},{7,4},{8,11},{9,10},{10,... | collective-permute-start | bytes 1376264 | tf_op jit(solution)/shard_map/ppermute | solution.py:375
  80.1 2.8 %collective-permute-start.12 = (f32[5,128,128]{2,1,0:T(8,128)S(1)}, f32[5,128,128]{2,1,0:T(8,128)S(1)}, u32[]{:S(2)}, u32[]{:S(2)}) collective-permute-start(f32[5,128,128]{2,1,0:T(8,128)S(1)} %get-tuple-element.31), channel_id=1, source_target_pairs={{0,4},{4,0},{1,5},{5,1},{2,6},{6,2},{3,7},{7,3},{8,12},{12,8},{9,1... | collective-permute-start | bytes 983048 | tf_op jit(solution)/shard_map/ppermute | solution.py:346
  98.1 2.7 %collective-permute-start.13 = (f32[40,128]{1,0:T(8,128)S(1)}, f32[40,128]{1,0:T(8,128)S(1)}, u32[]{:S(2)}, u32[]{:S(2)}) collective-permute-start(f32[40,128]{1,0:T(8,128)S(1)} %reduce_sum.9), channel_id=1, source_target_pairs={{0,1},{1,0},{2,3},{3,2},{4,5},{5,4},{6,7},{7,6},{8,9},{9,8},{10,11... | collective-permute-start | bytes 61448 | tf_op jit(solution)/shard_map/ppermute | solution.py:350
  100.8 4.3 %collective-permute-start.14 = (f32[40,128]{1,0:T(8,128)S(1)}, f32[40,128]{1,0:T(8,128)S(1)}, u32[]{:S(2)}, u32[]{:S(2)}) collective-permute-start(f32[40,128]{1,0:T(8,128)S(1)} %add.10), channel_id=1, source_target_pairs={{0,2},{1,3},{2,0},{3,1},{4,6},{5,7},{6,4},{7,5},{8,10},{9,11},{10,... | collective-permute-start | bytes 61448 | tf_op jit(solution)/shard_map/ppermute | solution.py:350
  116.5 6.5 %collective-permute-start.15 = (f32[5,128,128]{2,1,0:T(8,128)S(1)}, f32[5,128,128]{2,1,0:T(8,128)S(1)}, u32[]{:S(2)}, u32[]{:S(2)}) collective-permute-start(f32[5,128,128]{2,1,0:T(8,128)S(1)} %bitcast.8), channel_id=1, source_target_pairs={{0,4},{4,0},{1,5},{5,1},{2,6},{6,2},{3,7},{7,3},{8,12},{12,8},{9,1... | collective-permute-start | bytes 983048 | tf_op jit(solution)/shard_map/ppermute | solution.py:352

commit v3 on v2

--- a/solution.py
+++ b/solution.py
@@ -125,34 +125,22 @@
     )(ids, tiles)
 
 
-def world_kernel(w, ids_ref, cam_ref, e1_ref, e2_ref, e3_ref, r1_ref, r2_ref, r3_ref, mats_ref, coef_ref, *rest):
+def world_kernel(w, ids_ref, e0_ref, e1_ref, e2_ref, e3_ref, r0_ref, r1_ref, r2_ref, r3_ref, mats_ref, coef_ref, *rest):
     if w:
-        gin_ref, _, vel_out, mine_ref, other_ref, tiles, interp, vel_ref, sem, out_sem = rest
+        gin_ref, _, vel_out, mine_ref, other_ref, tiles, interp, vel_ref, out_sem = rest
     else:
-        vel_out, gram_ref, tiles, interp, vel_ref, sem, out_sem = rest
+        vel_out, gram_ref, tiles, interp, vel_ref, out_sem = rest
     _, cells, snaps = vel_ref.shape
-    firsts, others = (None, e1_ref, e2_ref, e3_ref), (None, r1_ref, r2_ref, r3_ref)
-    indices, dists = [], []
+    firsts, others = (e0_ref, e1_ref, e2_ref, e3_ref), (r0_ref, r1_ref, r2_ref, r3_ref)
     for c in range(2):
         tile = ids_ref[w, c]
         index, dist = tile & 3, lax.shift_right_logical(tile, 2) ^ lax.axis_index("x")
-        indices.append(index)
-        dists.append(dist)
-
-        @pl.when(dist == 0)
-        def _():
-            pltpu.make_async_copy(cam_ref.at[index], tiles.at[c], sem.at[c]).start()
-
-    for c in range(2):
         for k in range(4):
 
-            @pl.when(dists[c] == k)
+            @pl.when(dist == k)
             def _():
-                if k == 0:
-                    pltpu.make_async_copy(cam_ref.at[0], tiles.at[c], sem.at[c]).wait()
-                else:
-                    tiles[c, :, :EARLY] = firsts[k][indices[c]]
-                    tiles[c, :, EARLY:] = others[k][...]
+                tiles[c, :, :EARLY] = firsts[k][index]
+                tiles[c, :, EARLY:] = others[k][...]
 
         for j in range(2):
             interp[2 * c + j] = jnp.dot(mats_ref[w, c], tiles[c, j], preferred_element_type=F32)
@@ -168,11 +156,10 @@
             for i in range(1, 4):
                 total = total + coef_ref[q, at + i : at + i + 1] * parts[i]
             vel_ref[k, q, :] = total.astype(BF16)
+        pltpu.make_async_copy(vel_ref.at[:, q, :], vel_out.at[w, :, q, :], out_sem).start()
         return 0
 
     lax.fori_loop(0, cells // rows, cell_rows, 0)
-    leave = pltpu.make_async_copy(vel_ref, vel_out.at[w], out_sem)
-    leave.start()
     flat = vel_ref[...].reshape(3 * cells, snaps)
     core = lax.axis_index("core")
     for i in range(snaps // 256):
@@ -194,16 +181,16 @@
                 for half, at, part in parts:
                     (mine_ref if half == side else other_ref)[at] = part
 
-    leave.wait()
-
-
-def world(w, ids, cam, firsts, recv, mats, coef, carry):
-    snaps, cells = cam.shape[-1], mats.shape[2]
+    pltpu.make_async_copy(vel_ref, vel_out.at[w], out_sem).wait()
+
+
+def world(w, ids, firsts, recv, mats, coef, carry):
+    snaps, cells, pix = firsts[0].shape[-1], mats.shape[2], mats.shape[3]
     world_tiles = 2
     outs = 2 if w else 1
     grams = (len(HALVES[0]), 128, 128) if w else (2, len(HALVES[0]), 128, 128)
-    in_specs = [pl.BlockSpec(memory_space=pltpu.SMEM), ANY] + [VM] * 8
-    args = [ids, cam, *firsts, *recv, mats, coef]
+    in_specs = [pl.BlockSpec(memory_space=pltpu.SMEM)] + [VM] * 10
+    args = [ids, *firsts, *recv, mats, coef]
     aliases = {}
     if w:
         in_specs += [VM, ANY]
@@ -221,10 +208,9 @@
             *[jax.ShapeDtypeStruct(grams, F32)] * outs,
         ),
         scratch_shapes=[
-            pltpu.VMEM((2, 2, cam.shape[2], snaps), BF16),
+            pltpu.VMEM((2, 2, pix, snaps), BF16),
             pltpu.VMEM((4, cells, snaps), F32),
             pltpu.VMEM((3, cells, snaps), BF16),
-            pltpu.SemaphoreType.DMA((2,)),
             pltpu.SemaphoreType.DMA,
         ],
         input_output_aliases=aliases,
@@ -294,9 +280,12 @@
 
     o_ref[...] = jnp.zeros_like(o_ref)
 
-    def leave(q):
-        rows = pl.ds(q * size, size)
-        return pltpu.make_async_copy(o_ref.at[rows], out_ref.at[rows], sem.at[q])
+    def leave(q, zeros):
+        where = (pl.ds(q * size, size), pl.ds(0, q * size) if zeros else pl.ds(q * size, n - q * size))
+        return pltpu.make_async_copy(o_ref.at[where], out_ref.at[where], sem.at[int(zeros), q])
+
+    for q in range(1, parts):
+        leave(q, True).start()
 
     def panel(p, _):
         off = pl.multiple_of(p * size, size)
@@ -312,7 +301,7 @@
                 col = lax.broadcasted_iota(jnp.int32, (size, wide), 1)
                 r = jnp.where(col >= row, r, 0.0)
                 o_ref[lo : lo + size, lo:] = r
-                leave(q).start()
+                leave(q, False).start()
                 if q < parts - 1:
                     for m in range(q + 1, parts):
                         at = m * size
@@ -323,7 +312,9 @@
 
     lax.fori_loop(0, parts, panel, 0)
     for q in range(parts):
-        leave(q).wait()
+        leave(q, False).wait()
+        if q:
+            leave(q, True).wait()
 
 
 def factor(own, other, n):
@@ -332,7 +323,7 @@
         out_shape=jax.ShapeDtypeStruct((n, n), F32),
         in_specs=[VM, VM],
         out_specs=ANY,
-        scratch_shapes=[pltpu.VMEM((n, n), F32), pltpu.VMEM((n, n), F32), pltpu.SemaphoreType.DMA((n // 128,))],
+        scratch_shapes=[pltpu.VMEM((n, n), F32), pltpu.VMEM((n, n), F32), pltpu.SemaphoreType.DMA((2, n // 128))],
         compiler_params=pltpu.CompilerParams(vmem_limit_bytes=16 << 20),
         name="factor",
     )(own, other)
@@ -363,7 +354,7 @@
 
     swaps = [[(i, i ^ k) for i in range(groups)] for k in range(groups)]
     ids, sent = early(ids, tiles)
-    asked, firsts = [None], []
+    asked, firsts = [ids], [sent]
     for k in range(1, groups):
         asked.append(lax.ppermute(ids, "x", swaps[k]))
     for k in range(1, groups):
@@ -374,6 +365,9 @@
         for w in range(world_tiles):
             received[w][k] = lax.ppermute(payload[w], "x", swaps[k])
 
+    for w, tile in enumerate(select(ids, tiles)):
+        received[w][0] = tile
+
     mats, columns = prepare(
         stencil.reshape(world_tiles * 2, 2, cells),
         frac.reshape(world_tiles * 2, 2, cells),
@@ -383,7 +377,7 @@
 
     carry = None
     for w in range(world_tiles):
-        carry = world(w, ids, tiles, firsts, received[w][1:], mats, columns, carry)
+        carry = world(w, ids, firsts, received[w], mats, columns, carry)
     velocity, mine, other = carry
     total_rows = groups * lax.axis_size("y") * lax.axis_size("z") * 2 * world_tiles * 3 * cells
     halves = sum_devices(mine, other, F32(1.0 / total_rows))

time: 140 us -> 139 us (level)
  starting transfers between devices: 23.2 us -> 21.6 us
    pallas_call x3 -> x4, Pallas kernels: 5.19 us -> 6.93 us  [select(): pl.pallas_call(select_kernel, out_shape=[jax.ShapeDtypeStruct((parts, pix...]
    ppermute x6, waiting for transfers between devices: 30.6 us -> 29 us  [program(): received[w][k] = lax.ppermute(payload[w], 'x', swaps[k])]
  transfers between devices with their start and end apart: 16 -> 16, of which waited for: 10 -> 9; matrix products, arithmetic and copies ran while one was open for 0% -> 0% of each run, Pallas kernels for 6% -> 7%
where the time goes in v3:
time: 139 us
  waiting for transfers between devices  56.9 us (41%)
  Pallas kernels  32.3 us (23%)
  blocking collectives  27.2 us (20%)
  starting transfers between devices  21.6 us (16%)
    ppermute x6, waiting for transfers between devices, program(): received[w][k] = lax.ppermute(payload[w], 'x', swaps[k])  29 us
    ppermute x3, waiting for transfers between devices, program(): asked.append(lax.ppermute(ids, 'x', swaps[k]))  19.2 us
    pallas_call x1, Pallas kernels, factor(): pl.pallas_call(factor_kernel, out_shape=jax.ShapeDtypeStruct((n, n), F32)...  16.1 us
    all_to_all x1, blocking collectives, sum_devices(): pieces = lax.all_to_all(mine.reshape(planes, -1, 128), PLANE, 0, 0)  15.6 us
    all_to_all x1, blocking collectives, sum_devices(): lax.all_to_all(jnp.broadcast_to(piece * scale, pieces.shape), PLANE, 0, 0)  11.5 us
    pallas_call x4, Pallas kernels, select(): pl.pallas_call(select_kernel, out_shape=[jax.ShapeDtypeStruct((parts, pix...  6.93 us
    ppermute x6, starting transfers between devices, program(): received[w][k] = lax.ppermute(payload[w], 'x', swaps[k])  6.87 us
    pallas_call x2, Pallas kernels, world(): pl.pallas_call(functools.partial(world_kernel, w), in_specs=in_specs, out...  6.42 us
  transfers between devices with their start and end apart: 16, of which 9 were waited for; matrix products, arithmetic and copies ran while one was open for 0% of the time, Pallas kernels for 7%

profile of v3, /device:TPU:1, one launch (start us, length us, event | category | flops | bytes accessed | tf_op | source)
XLA Modules:
  0.0 139.1 jit_solution(12575550242442221908)
XLA Ops:
  0.6 1.0 early.1
  1.6 2.1 %collective-permute-start.3 = (s32[2,2]{1,0:T(2,128)S(1)}, s32[2,2]{1,0:T(2,128)S(1)}, u32[]{:S(2)}, u32[]{:S(2)}) collective-permute-start(s32[2,2]{1,0:T(2,128)S(1)} %get-tuple-element.19.ids_ref), channel_id=1, source_target_pairs={{0,1},{1,0},{2,3},{3,2},{4,5},{5,4},{6,7},{7,6},{8,9},{9,8},{10,11... | collective-permute-start | bytes 56 | tf_op jit(solution)/shard_map/ppermute | solution.py:359
  3.7 1.0 collective-permute-done.3.ids_ref
  4.7 1.7 %shard_map.69 = (bf16[2,224,512]{2,1,0:T(8,128)(2,1)S(1)}, bf16[2,224,512]{2,1,0:T(8,128)(2,1)S(1)}) custom-call(s32[2,2]{1,0:T(2,128)S(1)} %collective-permute-done.3.ids_ref, bf16[4,2,256,512]{3,2,1,0:T(8,128)(2,1)} %bitcast.13), custom_call_target="tpu_custom_call" | custom-call | bytes 2000000 | tf_op jit(solution)/shard_map/pallas_call | solution.py:117
  6.4 1.5 %collective-permute-start.9 = (bf16[2,224,512]{2,1,0:T(8,128)(2,1)S(1)}, bf16[2,224,512]{2,1,0:T(8,128)(2,1)S(1)}, u32[]{:S(2)}, u32[]{:S(2)}) collective-permute-start(bf16[2,224,512]{2,1,0:T(8,128)(2,1)S(1)} %get-tuple-element.28), channel_id=1, source_target_pairs={{0,1},{1,0},{2,3},{3,2},{4,5},{5,4},{6,7},{7,6},{8,9},{9,8},{10,11... | collective-permute-start | bytes 1376264 | tf_op jit(solution)/shard_map/ppermute | solution.py:366
  8.0 1.8 %collective-permute-start.2 = (bf16[4,2,32,512]{3,2,1,0:T(8,128)(2,1)S(1)}, bf16[4,2,32,512]{3,2,1,0:T(8,128)(2,1)S(1)}, u32[]{:S(2)}, u32[]{:S(2)}) collective-permute-start(bf16[4,2,32,512]{3,2,1,0:T(8,128)(2,1)S(1)} %get-tuple-element.20.e0_ref), channel_id=1, source_target_pairs={{0,3},{1,2},{2,1},{3,0},{4,7},{5,6},{6,5},{7,4},{8,11},{9,10},{10,... | collective-permute-start | bytes 786440 | tf_op jit(solution)/shard_map/ppermute | solution.py:361
  9.8 0.6 collective-permute-start.1
  10.4 0.8 collective-permute-start
  11.2 2.5 %collective-permute-start.5 = (s32[2,2]{1,0:T(2,128)S(1)}, s32[2,2]{1,0:T(2,128)S(1)}, u32[]{:S(2)}, u32[]{:S(2)}) collective-permute-start(s32[2,2]{1,0:T(2,128)S(1)} %get-tuple-element.19.ids_ref), channel_id=1, source_target_pairs={{0,2},{1,3},{2,0},{3,1},{4,6},{5,7},{6,4},{7,5},{8,10},{9,11},{10,... | collective-permute-start | bytes 56 | tf_op jit(solution)/shard_map/ppermute | solution.py:359
  13.7 16.4 %collective-permute-done.5.ids_ref = s32[2,2]{1,0:T(2,128)S(1)} collective-permute-done((s32[2,2]{1,0:T(2,128)S(1)}, s32[2,2]{1,0:T(2,128)S(1)}, u32[]{:S(2)}, u32[]{:S(2)}) %collective-permute-start.5) | collective-permute-done | bytes 48 | tf_op jit(solution)/shard_map/ppermute | solution.py:359
  30.1 0.0 collective-permute-start.7
  30.1 1.7 %shard_map.70 = (bf16[2,224,512]{2,1,0:T(8,128)(2,1)S(1)}, bf16[2,224,512]{2,1,0:T(8,128)(2,1)S(1)}) custom-call(s32[2,2]{1,0:T(2,128)S(1)} %collective-permute-done.5.ids_ref, bf16[4,2,256,512]{3,2,1,0:T(8,128)(2,1)} %bitcast.14), custom_call_target="tpu_custom_call" | custom-call | bytes 2000000 | tf_op jit(solution)/shard_map/pallas_call | solution.py:117
  31.8 1.9 %collective-permute-done.7.ids_ref = s32[2,2]{1,0:T(2,128)S(1)} collective-permute-done((s32[2,2]{1,0:T(2,128)S(1)}, s32[2,2]{1,0:T(2,128)S(1)}, u32[]{:S(2)}, u32[]{:S(2)}) %collective-permute-start.7) | collective-permute-done | bytes 48 | tf_op jit(solution)/shard_map/ppermute | solution.py:359
  33.7 0.0 collective-permute-start.10
  33.7 1.7 %shard_map.71 = (bf16[2,224,512]{2,1,0:T(8,128)(2,1)S(1)}, bf16[2,224,512]{2,1,0:T(8,128)(2,1)S(1)}) custom-call(s32[2,2]{1,0:T(2,128)S(1)} %collective-permute-done.7.ids_ref, bf16[4,2,256,512]{3,2,1,0:T(8,128)(2,1)} %bitcast.15), custom_call_target="tpu_custom_call" | custom-call | bytes 2000000 | tf_op jit(solution)/shard_map/pallas_call | solution.py:117
  35.5 0.0 copy-start.2
  35.5 0.0 copy-start
  35.5 0.0 copy-start.1
  35.5 0.0 collective-permute-done.2.e3_ref
  35.5 1.4 %collective-permute-start.11 = (bf16[2,224,512]{2,1,0:T(8,128)(2,1)S(1)}, bf16[2,224,512]{2,1,0:T(8,128)(2,1)S(1)}, u32[]{:S(2)}, u32[]{:S(2)}) collective-permute-start(bf16[2,224,512]{2,1,0:T(8,128)(2,1)S(1)} %get-tuple-element.30), channel_id=1, source_target_pairs={{0,3},{1,2},{2,1},{3,0},{4,7},{5,6},{6,5},{7,4},{8,11},{9,10},{10,... | collective-permute-start | bytes 1376264 | tf_op jit(solution)/shard_map/ppermute | solution.py:366
  37.0 0.0 collective-permute-done.1.e2_ref
  37.0 1.3 collective-permute-start.4
  38.2 0.0 collective-permute-done.e1_ref
  38.2 1.2 collective-permute-start.6
  39.5 0.0 collective-permute-done.9.r1_ref
  39.5 1.4 collective-permute-start.8
  40.8 1.7 %shard_map.68 = (bf16[2,224,512]{2,1,0:T(8,128)(2,1)S(1)}, bf16[2,224,512]{2,1,0:T(8,128)(2,1)S(1)}) custom-call(s32[2,2]{1,0:T(2,128)S(1)} %get-tuple-element.19.ids_ref, bf16[4,2,256,512]{3,2,1,0:T(8,128)(2,1)} %bitcast.16), custom_call_target="tpu_custom_call" | custom-call | bytes 2000000 | tf_op jit(solution)/shard_map/pallas_call | solution.py:117
  42.6 0.0 copy-done.2
  42.6 0.0 copy-done
  42.6 0.0 copy-done.1
  42.6 1.9 %prepare.1 = (bf16[2,2,256,256]{3,2,1,0:T(8,128)(2,1)S(1)}, f32[256,128]{1,0:T(8,128)S(1)}) custom-call(s32[4,2,256]{2,1,0:T(2,128)S(1)} %bitcast.10, f32[4,2,256]{2,1,0:T(2,128)S(1)} %bitcast.11, f32[2,12,256]{2,1,0:T(8,128)S(1)} %copy.9.coef_ref), custom_call_target="tpu_custom_call" | custom-call | flops 4000000 | bytes 1000000 | tf_op jit(solution)/shard_map/prepare/pallas_call | solution.py:60
  44.5 0.0 collective-permute-done.10.r2_ref
  44.5 16.5 %collective-permute-done.11.r3_ref = bf16[2,224,512]{2,1,0:T(8,128)(2,1)S(1)} collective-permute-done((bf16[2,224,512]{2,1,0:T(8,128)(2,1)S(1)}, bf16[2,224,512]{2,1,0:T(8,128)(2,1)S(1)}, u32[]{:S(2)}, u32[]{:S(2)}) %collective-permute-start.11) | collective-permute-done | bytes 458784 | tf_op jit(solution)/shard_map/ppermute | solution.py:366
  61.0 3.1 %shard_map.72 = (bf16[2,3,256,512]{3,2,1,0:T(8,128)(2,1)}, f32[2,5,128,128]{3,2,1,0:T(8,128)S(1)}) custom-call(s32[2,2]{1,0:T(2,128)S(1)} %get-tuple-element.19.ids_ref, bf16[4,2,32,512]{3,2,1,0:T(8,128)(2,1)S(1)} %get-tuple-element.20.e0_ref, bf16[4,2,32,512]{3,2,1,0:T(8,128)(2,1)S(1)} %collective-permute-done.e1_ref, ...), custom_call_target="tpu_custom_call" | custom-call | flops 700000000 | bytes 4000000 | tf_op jit(solution)/shard_map/pallas_call | solution.py:199
  64.2 0.0 collective-permute-done.4.r1_ref
  64.2 0.0 collective-permute-done.6.r2_ref
  64.2 12.5 %collective-permute-done.8.r3_ref = bf16[2,224,512]{2,1,0:T(8,128)(2,1)S(1)} collective-permute-done((bf16[2,224,512]{2,1,0:T(8,128)(2,1)S(1)}, bf16[2,224,512]{2,1,0:T(8,128)(2,1)S(1)}, u32[]{:S(2)}, u32[]{:S(2)}) %collective-permute-start.8) | collective-permute-done | bytes 458784 | tf_op jit(solution)/shard_map/ppermute | solution.py:366
  76.7 3.3 %shard_map.73 = (bf16[2,3,256,512]{3,2,1,0:T(8,128)(2,1)}, f32[5,128,128]{2,1,0:T(8,128)S(1)}, f32[5,128,128]{2,1,0:T(8,128)S(1)}) custom-call(s32[2,2]{1,0:T(2,128)S(1)} %get-tuple-element.19.ids_ref, bf16[4,2,32,512]{3,2,1,0:T(8,128)(2,1)S(1)} %get-tuple-element.20.e0_ref, ...), custom_call_target="tpu_custom_call", output_to_operand_aliasing={{0}: (12, {})} | custom-call | flops 700000000 | bytes 4000000 | tf_op jit(solution)/shard_map/pallas_call | solution.py:199
  80.0 1.0 collective-permute-start.12
  81.0 1.3 collective-permute-done.12
  82.3 15.6 %all_to_all.10 = f32[16,40,128]{2,1,0:T(8,128)S(1)} all-to-all(f32[16,40,128]{2,1,0:T(8,128)S(1)} %bitcast.18), channel_id=1, replica_groups=mesh['y'=4,'z'=4,'core'=2,'x'=4] {'y','z'}, dimensions={0} | all-to-all | bytes 655360 | tf_op jit(solution)/shard_map/all_to_all | solution.py:338
  97.9 0.1 collective-permute-start.13
  98.0 2.6 %collective-permute-done.13 = f32[40,128]{1,0:T(8,128)S(1)} collective-permute-done((f32[40,128]{1,0:T(8,128)S(1)}, f32[40,128]{1,0:T(8,128)S(1)}, u32[]{:S(2)}, u32[]{:S(2)}) %collective-permute-start.13) | collective-permute-done | bytes 20512 | tf_op jit(solution)/shard_map/ppermute | solution.py:341
  100.7 0.6 collective-permute-start.14
  101.3 3.5 %collective-permute-done.14 = f32[40,128]{1,0:T(8,128)S(1)} collective-permute-done((f32[40,128]{1,0:T(8,128)S(1)}, f32[40,128]{1,0:T(8,128)S(1)}, u32[]{:S(2)}, u32[]{:S(2)}) %collective-permute-start.14) | collective-permute-done | bytes 20512 | tf_op jit(solution)/shard_map/ppermute | solution.py:341
  104.8 11.5 %all_to_all.11 = f32[16,40,128]{2,1,0:T(8,128)S(1)} all-to-all(f32[16,40,128]{2,1,0:T(8,128)S(1)} %broadcast_in_dim.3), channel_id=1, replica_groups=mesh['y'=4,'z'=4,'core'=2,'x'=4] {'y','z'}, dimensions={0} | all-to-all | bytes 655360 | tf_op jit(solution)/shard_map/all_to_all | solution.py:342
  116.4 5.2 %collective-permute-start.15 = (f32[5,128,128]{2,1,0:T(8,128)S(1)}, f32[5,128,128]{2,1,0:T(8,128)S(1)}, u32[]{:S(2)}, u32[]{:S(2)}) collective-permute-start(f32[5,128,128]{2,1,0:T(8,128)S(1)} %bitcast.8), channel_id=1, source_target_pairs={{0,4},{4,0},{1,5},{5,1},{2,6},{6,2},{3,7},{7,3},{8,12},{12,8},{9,1... | collective-permute-start | bytes 983048 | tf_op jit(solution)/shard_map/ppermute | solution.py:343
  121.6 1.3 collective-permute-done.15.other_ref
  122.9 16.1 %factor.1 = f32[512,512]{1,0:T(8,128)} custom-call(f32[5,128,128]{2,1,0:T(8,128)S(1)} %bitcast.9, f32[5,128,128]{2,1,0:T(8,128)S(1)} %collective-permute-done.15.other_ref), custom_call_target="tpu_custom_call" | custom-call | tf_op jit(solution)/shard_map/factor/pallas_call | solution.py:321
  (7 shorter events, 0.1 us)
Async XLA Ops:
  1.6 3.1 %collective-permute-start.3 = (s32[2,2]{1,0:T(2,128)S(1)}, s32[2,2]{1,0:T(2,128)S(1)}, u32[]{:S(2)}, u32[]{:S(2)}) collective-permute-start(s32[2,2]{1,0:T(2,128)S(1)} %get-tuple-element.19.ids_ref), channel_id=1, source_target_pairs={{0,1},{1,0},{2,3},{3,2},{4,5},{5,4},{6,7},{7,6},{8,9},{9,8},{10,11... | collective-permute-start | bytes 56 | tf_op jit(solution)/shard_map/ppermute | solution.py:359
  6.4 33.0 %collective-permute-start.9 = (bf16[2,224,512]{2,1,0:T(8,128)(2,1)S(1)}, bf16[2,224,512]{2,1,0:T(8,128)(2,1)S(1)}, u32[]{:S(2)}, u32[]{:S(2)}) collective-permute-start(bf16[2,224,512]{2,1,0:T(8,128)(2,1)S(1)} %get-tuple-element.28), channel_id=1, source_target_pairs={{0,1},{1,0},{2,3},{3,2},{4,5},{5,4},{6,7},{7,6},{8,9},{9,8},{10,11... | collective-permute-start | bytes 1376264 | tf_op jit(solution)/shard_map/ppermute | solution.py:366
  8.0 27.5 %collective-permute-start.2 = (bf16[4,2,32,512]{3,2,1,0:T(8,128)(2,1)S(1)}, bf16[4,2,32,512]{3,2,1,0:T(8,128)(2,1)S(1)}, u32[]{:S(2)}, u32[]{:S(2)}) collective-permute-start(bf16[4,2,32,512]{3,2,1,0:T(8,128)(2,1)S(1)} %get-tuple-element.20.e0_ref), channel_id=1, source_target_pairs={{0,3},{1,2},{2,1},{3,0},{4,7},{5,6},{6,5},{7,4},{8,11},{9,10},{10,... | collective-permute-start | bytes 786440 | tf_op jit(solution)/shard_map/ppermute | solution.py:361
  9.8 27.2 %collective-permute-start.1 = (bf16[4,2,32,512]{3,2,1,0:T(8,128)(2,1)S(1)}, bf16[4,2,32,512]{3,2,1,0:T(8,128)(2,1)S(1)}, u32[]{:S(2)}, u32[]{:S(2)}) collective-permute-start(bf16[4,2,32,512]{3,2,1,0:T(8,128)(2,1)S(1)} %get-tuple-element.20.e0_ref), channel_id=1, source_target_pairs={{0,2},{1,3},{2,0},{3,1},{4,6},{5,7},{6,4},{7,5},{8,10},{9,11},{10,... | collective-permute-start | bytes 786440 | tf_op jit(solution)/shard_map/ppermute | solution.py:361
  10.4 27.8 %collective-permute-start = (bf16[4,2,32,512]{3,2,1,0:T(8,128)(2,1)S(1)}, bf16[4,2,32,512]{3,2,1,0:T(8,128)(2,1)S(1)}, u32[]{:S(2)}, u32[]{:S(2)}) collective-permute-start(bf16[4,2,32,512]{3,2,1,0:T(8,128)(2,1)S(1)} %get-tuple-element.20.e0_ref), channel_id=1, source_target_pairs={{0,1},{1,0},{2,3},{3,2},{4,5},{5,4},{6,7},{7,6},{8,9},{9,8},{10,11... | collective-permute-start | bytes 786440 | tf_op jit(solution)/shard_map/ppermute | solution.py:361
  11.2 18.8 %collective-permute-start.5 = (s32[2,2]{1,0:T(2,128)S(1)}, s32[2,2]{1,0:T(2,128)S(1)}, u32[]{:S(2)}, u32[]{:S(2)}) collective-permute-start(s32[2,2]{1,0:T(2,128)S(1)} %get-tuple-element.19.ids_ref), channel_id=1, source_target_pairs={{0,2},{1,3},{2,0},{3,1},{4,6},{5,7},{6,4},{7,5},{8,10},{9,11},{10,... | collective-permute-start | bytes 56 | tf_op jit(solution)/shard_map/ppermute | solution.py:359
  30.1 3.6 %collective-permute-start.7 = (s32[2,2]{1,0:T(2,128)S(1)}, s32[2,2]{1,0:T(2,128)S(1)}, u32[]{:S(2)}, u32[]{:S(2)}) collective-permute-start(s32[2,2]{1,0:T(2,128)S(1)} %get-tuple-element.19.ids_ref), channel_id=1, source_target_pairs={{0,3},{1,2},{2,1},{3,0},{4,7},{5,6},{6,5},{7,4},{8,11},{9,10},{10,... | collective-permute-start | bytes 56 | tf_op jit(solution)/shard_map/ppermute | solution.py:359
  33.7 10.8 %collective-permute-start.10 = (bf16[2,224,512]{2,1,0:T(8,128)(2,1)S(1)}, bf16[2,224,512]{2,1,0:T(8,128)(2,1)S(1)}, u32[]{:S(2)}, u32[]{:S(2)}) collective-permute-start(bf16[2,224,512]{2,1,0:T(8,128)(2,1)S(1)} %get-tuple-element.29), channel_id=1, source_target_pairs={{0,2},{1,3},{2,0},{3,1},{4,6},{5,7},{6,4},{7,5},{8,10},{9,11},{10,... | collective-permute-start | bytes 1376264 | tf_op jit(solution)/shard_map/ppermute | solution.py:366
  35.5 7.1 %copy-start.2 = (f32[1,1,2,3,4,256]{5,4,3,2,1,0:T(4,128)S(1)}, f32[1,1,2,3,4,256]{5,4,3,2,1,0:T(4,128)}, u32[]{:S(2)}) copy-start(f32[1,1,2,3,4,256]{5,4,3,2,1,0:T(4,128)} %param.9) | copy-start | bytes 73732
  35.5 7.1 %copy-start = (s32[1,1,2,2,2,256]{5,4,3,2,1,0:T(2,128)S(1)}, s32[1,1,2,2,2,256]{5,4,3,2,1,0:T(2,128)}, u32[]{:S(2)}) copy-start(s32[1,1,2,2,2,256]{5,4,3,2,1,0:T(2,128)} %param.7) | copy-start | bytes 24580
  35.5 7.1 %copy-start.1 = (f32[1,1,2,2,2,256]{5,4,3,2,1,0:T(2,128)S(1)}, f32[1,1,2,2,2,256]{5,4,3,2,1,0:T(2,128)}, u32[]{:S(2)}) copy-start(f32[1,1,2,2,2,256]{5,4,3,2,1,0:T(2,128)} %param.8) | copy-start | bytes 24580
  35.5 25.5 %collective-permute-start.11 = (bf16[2,224,512]{2,1,0:T(8,128)(2,1)S(1)}, bf16[2,224,512]{2,1,0:T(8,128)(2,1)S(1)}, u32[]{:S(2)}, u32[]{:S(2)}) collective-permute-start(bf16[2,224,512]{2,1,0:T(8,128)(2,1)S(1)} %get-tuple-element.30), channel_id=1, source_target_pairs={{0,3},{1,2},{2,1},{3,0},{4,7},{5,6},{6,5},{7,4},{8,11},{9,10},{10,... | collective-permute-start | bytes 1376264 | tf_op jit(solution)/shard_map/ppermute | solution.py:366
  37.0 27.2 %collective-permute-start.4 = (bf16[2,224,512]{2,1,0:T(8,128)(2,1)S(1)}, bf16[2,224,512]{2,1,0:T(8,128)(2,1)S(1)}, u32[]{:S(2)}, u32[]{:S(2)}) collective-permute-start(bf16[2,224,512]{2,1,0:T(8,128)(2,1)S(1)} %get-tuple-element.22), channel_id=1, source_target_pairs={{0,1},{1,0},{2,3},{3,2},{4,5},{5,4},{6,7},{7,6},{8,9},{9,8},{10,11... | collective-permute-start | bytes 1376264 | tf_op jit(solution)/shard_map/ppermute | solution.py:366
  38.2 26.0 %collective-permute-start.6 = (bf16[2,224,512]{2,1,0:T(8,128)(2,1)S(1)}, bf16[2,224,512]{2,1,0:T(8,128)(2,1)S(1)}, u32[]{:S(2)}, u32[]{:S(2)}) collective-permute-start(bf16[2,224,512]{2,1,0:T(8,128)(2,1)S(1)} %get-tuple-element.23), channel_id=1, source_target_pairs={{0,2},{1,3},{2,0},{3,1},{4,6},{5,7},{6,4},{7,5},{8,10},{9,11},{10,... | collective-permute-start | bytes 1376264 | tf_op jit(solution)/shard_map/ppermute | solution.py:366
  39.5 37.2 %collective-permute-start.8 = (bf16[2,224,512]{2,1,0:T(8,128)(2,1)S(1)}, bf16[2,224,512]{2,1,0:T(8,128)(2,1)S(1)}, u32[]{:S(2)}, u32[]{:S(2)}) collective-permute-start(bf16[2,224,512]{2,1,0:T(8,128)(2,1)S(1)} %get-tuple-element.24), channel_id=1, source_target_pairs={{0,3},{1,2},{2,1},{3,0},{4,7},{5,6},{6,5},{7,4},{8,11},{9,10},{10,... | collective-permute-start | bytes 1376264 | tf_op jit(solution)/shard_map/ppermute | solution.py:366
  80.0 2.2 %collective-permute-start.12 = (f32[5,128,128]{2,1,0:T(8,128)S(1)}, f32[5,128,128]{2,1,0:T(8,128)S(1)}, u32[]{:S(2)}, u32[]{:S(2)}) collective-permute-start(f32[5,128,128]{2,1,0:T(8,128)S(1)} %get-tuple-element.35), channel_id=1, source_target_pairs={{0,4},{4,0},{1,5},{5,1},{2,6},{6,2},{3,7},{7,3},{8,12},{12,8},{9,1... | collective-permute-start | bytes 983048 | tf_op jit(solution)/shard_map/ppermute | solution.py:337
  97.9 2.7 %collective-permute-start.13 = (f32[40,128]{1,0:T(8,128)S(1)}, f32[40,128]{1,0:T(8,128)S(1)}, u32[]{:S(2)}, u32[]{:S(2)}) collective-permute-start(f32[40,128]{1,0:T(8,128)S(1)} %reduce_sum.9), channel_id=1, source_target_pairs={{0,1},{1,0},{2,3},{3,2},{4,5},{5,4},{6,7},{7,6},{8,9},{9,8},{10,11... | collective-permute-start | bytes 61448 | tf_op jit(solution)/shard_map/ppermute | solution.py:341
  100.7 4.1 %collective-permute-start.14 = (f32[40,128]{1,0:T(8,128)S(1)}, f32[40,128]{1,0:T(8,128)S(1)}, u32[]{:S(2)}, u32[]{:S(2)}) collective-permute-start(f32[40,128]{1,0:T(8,128)S(1)} %add.10), channel_id=1, source_target_pairs={{0,2},{1,3},{2,0},{3,1},{4,6},{5,7},{6,4},{7,5},{8,10},{9,11},{10,... | collective-permute-start | bytes 61448 | tf_op jit(solution)/shard_map/ppermute | solution.py:341
  116.4 6.5 %collective-permute-start.15 = (f32[5,128,128]{2,1,0:T(8,128)S(1)}, f32[5,128,128]{2,1,0:T(8,128)S(1)}, u32[]{:S(2)}, u32[]{:S(2)}) collective-permute-start(f32[5,128,128]{2,1,0:T(8,128)S(1)} %bitcast.8), channel_id=1, source_target_pairs={{0,4},{4,0},{1,5},{5,1},{2,6},{6,2},{3,7},{7,3},{8,12},{12,8},{9,1... | collective-permute-start | bytes 983048 | tf_op jit(solution)/shard_map/ppermute | solution.py:343

commit v4 on v3

--- a/solution.py
+++ b/solution.py
@@ -11,7 +11,7 @@
 F32 = jnp.float32
 BF16 = jnp.bfloat16
 TILE_SIDE = 16
-EARLY = 32
+EARLY = 16
 HALVES = (((0, 3), (1, 3), (2, 3), (3, 3), (0, 0)), ((0, 2), (1, 2), (2, 2), (0, 1), (1, 1)))
 PLACE = {block: (half, at) for half, blocks in enumerate(HALVES) for at, block in enumerate(blocks)}
 PLANE = ("y", "z")
@@ -236,6 +236,7 @@
         inside = (lane >= k0) & (lane < k0 + size)
         rows = [jnp.where(inside, jnp.where(lane - k0 - 8 * v == sub, 1.0, 0.0), a) for v, a in enumerate(own)]
         scaled = [None] * per
+        diagonal = spread(columns[0][0], 0)
         for k in range(size):
             at, here = k // 8, is_row[k % 8]
 
@@ -243,7 +244,10 @@
                 return [jnp.where(here, value, x) if v == at else x for v, x in enumerate(parts)]
 
             pivot, row = fill(columns[k], -1.0), spread(rows[at], k)
-            root = lax.rsqrt(spread(columns[k][at], k))
+            root = lax.rsqrt(diagonal)
+            if k + 1 < size:
+                below, v = spread(columns[k][(k + 1) // 8], k + 1) * root, (k + 1) // 8
+                diagonal = spread(columns[k + 1][v], k + 1) - below * below
             pivot = [x * root for x in pivot]
             final = row * root
             scaled[at] = final if scaled[at] is None else jnp.where(here, final, scaled[at])

time: 139 us -> 137 us (0.986)
    ppermute x3, waiting for transfers between devices: 19.2 us -> 14.6 us  [program(): asked.append(lax.ppermute(ids, 'x', swaps[k]))]
    ppermute x6, waiting for transfers between devices: 29 us -> 32.4 us  [program(): received[w][k] = lax.ppermute(payload[w], 'x', swaps[k])]
where the time goes in v4:
time: 137 us
  waiting for transfers between devices  55.6 us (41%)
  Pallas kernels  32.1 us (23%)
  blocking collectives  27.2 us (20%)
  starting transfers between devices  21 us (15%)
    ppermute x6, waiting for transfers between devices, program(): received[w][k] = lax.ppermute(payload[w], 'x', swaps[k])  32.4 us
    pallas_call x1, Pallas kernels, factor(): pl.pallas_call(factor_kernel, out_shape=jax.ShapeDtypeStruct((n, n), F32)...  16 us
    all_to_all x1, blocking collectives, sum_devices(): pieces = lax.all_to_all(mine.reshape(planes, -1, 128), PLANE, 0, 0)  15.7 us
    ppermute x3, waiting for transfers between devices, program(): asked.append(lax.ppermute(ids, 'x', swaps[k]))  14.6 us
    all_to_all x1, blocking collectives, sum_devices(): lax.all_to_all(jnp.broadcast_to(piece * scale, pieces.shape), PLANE, 0, 0)  11.5 us
    pallas_call x4, Pallas kernels, select(): pl.pallas_call(select_kernel, out_shape=[jax.ShapeDtypeStruct((parts, pix...  7.01 us
    ppermute x6, starting transfers between devices, program(): received[w][k] = lax.ppermute(payload[w], 'x', swaps[k])  6.75 us
    pallas_call x2, Pallas kernels, world(): pl.pallas_call(functools.partial(world_kernel, w), in_specs=in_specs, out...  6.41 us
  transfers between devices with their start and end apart: 16, of which 9 were waited for; matrix products, arithmetic and copies ran while one was open for 0% of the time, Pallas kernels for 7%

profile of v4, /device:TPU:1, one launch (start us, length us, event | category | flops | bytes accessed | tf_op | source)
XLA Modules:
  0.0 137.1 jit_solution(10385299088230471102)
XLA Ops:
  0.6 0.9 early.1
  1.5 2.1 %collective-permute-start.3 = (s32[2,2]{1,0:T(2,128)S(1)}, s32[2,2]{1,0:T(2,128)S(1)}, u32[]{:S(2)}, u32[]{:S(2)}) collective-permute-start(s32[2,2]{1,0:T(2,128)S(1)} %get-tuple-element.19.ids_ref), channel_id=1, source_target_pairs={{0,1},{1,0},{2,3},{3,2},{4,5},{5,4},{6,7},{7,6},{8,9},{9,8},{10,11... | collective-permute-start | bytes 56 | tf_op jit(solution)/shard_map/ppermute | solution.py:363
  3.6 1.0 collective-permute-done.3.ids_ref
  4.6 1.8 %shard_map.69 = (bf16[2,240,512]{2,1,0:T(8,128)(2,1)S(1)}, bf16[2,240,512]{2,1,0:T(8,128)(2,1)S(1)}) custom-call(s32[2,2]{1,0:T(2,128)S(1)} %collective-permute-done.3.ids_ref, bf16[4,2,256,512]{3,2,1,0:T(8,128)(2,1)} %bitcast.13), custom_call_target="tpu_custom_call" | custom-call | bytes 2000000 | tf_op jit(solution)/shard_map/pallas_call | solution.py:117
  6.3 1.5 %collective-permute-start.9 = (bf16[2,240,512]{2,1,0:T(8,128)(2,1)S(1)}, bf16[2,240,512]{2,1,0:T(8,128)(2,1)S(1)}, u32[]{:S(2)}, u32[]{:S(2)}) collective-permute-start(bf16[2,240,512]{2,1,0:T(8,128)(2,1)S(1)} %get-tuple-element.28), channel_id=1, source_target_pairs={{0,1},{1,0},{2,3},{3,2},{4,5},{5,4},{6,7},{7,6},{8,9},{9,8},{10,11... | collective-permute-start | bytes 1474568 | tf_op jit(solution)/shard_map/ppermute | solution.py:370
  7.9 1.8 %collective-permute-start.2 = (bf16[4,2,16,512]{3,2,1,0:T(8,128)(2,1)S(1)}, bf16[4,2,16,512]{3,2,1,0:T(8,128)(2,1)S(1)}, u32[]{:S(2)}, u32[]{:S(2)}) collective-permute-start(bf16[4,2,16,512]{3,2,1,0:T(8,128)(2,1)S(1)} %get-tuple-element.20.e0_ref), channel_id=1, source_target_pairs={{0,3},{1,2},{2,1},{3,0},{4,7},{5,6},{6,5},{7,4},{8,11},{9,10},{10,... | collective-permute-start | bytes 393224 | tf_op jit(solution)/shard_map/ppermute | solution.py:365
  9.7 0.6 collective-permute-start.1
  10.3 0.8 collective-permute-start
  11.1 2.5 %collective-permute-start.5 = (s32[2,2]{1,0:T(2,128)S(1)}, s32[2,2]{1,0:T(2,128)S(1)}, u32[]{:S(2)}, u32[]{:S(2)}) collective-permute-start(s32[2,2]{1,0:T(2,128)S(1)} %get-tuple-element.19.ids_ref), channel_id=1, source_target_pairs={{0,2},{1,3},{2,0},{3,1},{4,6},{5,7},{6,4},{7,5},{8,10},{9,11},{10,... | collective-permute-start | bytes 56 | tf_op jit(solution)/shard_map/ppermute | solution.py:363
  13.6 11.7 %collective-permute-done.5.ids_ref = s32[2,2]{1,0:T(2,128)S(1)} collective-permute-done((s32[2,2]{1,0:T(2,128)S(1)}, s32[2,2]{1,0:T(2,128)S(1)}, u32[]{:S(2)}, u32[]{:S(2)}) %collective-permute-start.5) | collective-permute-done | bytes 48 | tf_op jit(solution)/shard_map/ppermute | solution.py:363
  25.3 0.0 collective-permute-start.7
  25.3 1.8 %shard_map.70 = (bf16[2,240,512]{2,1,0:T(8,128)(2,1)S(1)}, bf16[2,240,512]{2,1,0:T(8,128)(2,1)S(1)}) custom-call(s32[2,2]{1,0:T(2,128)S(1)} %collective-permute-done.5.ids_ref, bf16[4,2,256,512]{3,2,1,0:T(8,128)(2,1)} %bitcast.14), custom_call_target="tpu_custom_call" | custom-call | bytes 2000000 | tf_op jit(solution)/shard_map/pallas_call | solution.py:117
  27.1 1.9 %collective-permute-done.7.ids_ref = s32[2,2]{1,0:T(2,128)S(1)} collective-permute-done((s32[2,2]{1,0:T(2,128)S(1)}, s32[2,2]{1,0:T(2,128)S(1)}, u32[]{:S(2)}, u32[]{:S(2)}) %collective-permute-start.7) | collective-permute-done | bytes 48 | tf_op jit(solution)/shard_map/ppermute | solution.py:363
  28.9 0.1 collective-permute-start.10
  29.0 1.8 %shard_map.71 = (bf16[2,240,512]{2,1,0:T(8,128)(2,1)S(1)}, bf16[2,240,512]{2,1,0:T(8,128)(2,1)S(1)}) custom-call(s32[2,2]{1,0:T(2,128)S(1)} %collective-permute-done.7.ids_ref, bf16[4,2,256,512]{3,2,1,0:T(8,128)(2,1)} %bitcast.15), custom_call_target="tpu_custom_call" | custom-call | bytes 2000000 | tf_op jit(solution)/shard_map/pallas_call | solution.py:117
  30.8 0.0 copy-start.2
  30.8 0.0 copy-start
  30.8 0.0 copy-start.1
  30.8 0.0 collective-permute-done.2.e3_ref
  30.8 1.3 collective-permute-start.11
  32.1 0.0 collective-permute-done.1.e2_ref
  32.1 1.4 %collective-permute-start.4 = (bf16[2,240,512]{2,1,0:T(8,128)(2,1)S(1)}, bf16[2,240,512]{2,1,0:T(8,128)(2,1)S(1)}, u32[]{:S(2)}, u32[]{:S(2)}) collective-permute-start(bf16[2,240,512]{2,1,0:T(8,128)(2,1)S(1)} %get-tuple-element.22), channel_id=1, source_target_pairs={{0,1},{1,0},{2,3},{3,2},{4,5},{5,4},{6,7},{7,6},{8,9},{9,8},{10,11... | collective-permute-start | bytes 1474568 | tf_op jit(solution)/shard_map/ppermute | solution.py:370
  33.5 0.0 collective-permute-done.e1_ref
  33.5 1.3 collective-permute-start.6
  34.8 0.0 collective-permute-done.9.r1_ref
  34.8 1.2 collective-permute-start.8
  36.0 1.8 %shard_map.68 = (bf16[2,240,512]{2,1,0:T(8,128)(2,1)S(1)}, bf16[2,240,512]{2,1,0:T(8,128)(2,1)S(1)}) custom-call(s32[2,2]{1,0:T(2,128)S(1)} %get-tuple-element.19.ids_ref, bf16[4,2,256,512]{3,2,1,0:T(8,128)(2,1)} %bitcast.16), custom_call_target="tpu_custom_call" | custom-call | bytes 2000000 | tf_op jit(solution)/shard_map/pallas_call | solution.py:117
  37.7 0.0 copy-done.2
  37.8 0.0 copy-done
  37.8 0.0 copy-done.1
  37.8 1.9 %prepare.1 = (bf16[2,2,256,256]{3,2,1,0:T(8,128)(2,1)S(1)}, f32[256,128]{1,0:T(8,128)S(1)}) custom-call(s32[4,2,256]{2,1,0:T(2,128)S(1)} %bitcast.10, f32[4,2,256]{2,1,0:T(2,128)S(1)} %bitcast.11, f32[2,12,256]{2,1,0:T(8,128)S(1)} %copy.9.coef_ref), custom_call_target="tpu_custom_call" | custom-call | flops 4000000 | bytes 1000000 | tf_op jit(solution)/shard_map/prepare/pallas_call | solution.py:60
  39.7 0.0 collective-permute-done.10.r2_ref
  39.7 18.7 %collective-permute-done.11.r3_ref = bf16[2,240,512]{2,1,0:T(8,128)(2,1)S(1)} collective-permute-done((bf16[2,240,512]{2,1,0:T(8,128)(2,1)S(1)}, bf16[2,240,512]{2,1,0:T(8,128)(2,1)S(1)}, u32[]{:S(2)}, u32[]{:S(2)}) %collective-permute-start.11) | collective-permute-done | bytes 491552 | tf_op jit(solution)/shard_map/ppermute | solution.py:370
  58.4 3.1 %shard_map.72 = (bf16[2,3,256,512]{3,2,1,0:T(8,128)(2,1)}, f32[2,5,128,128]{3,2,1,0:T(8,128)S(1)}) custom-call(s32[2,2]{1,0:T(2,128)S(1)} %get-tuple-element.19.ids_ref, bf16[4,2,16,512]{3,2,1,0:T(8,128)(2,1)S(1)} %get-tuple-element.20.e0_ref, bf16[4,2,16,512]{3,2,1,0:T(8,128)(2,1)S(1)} %collective-permute-done.e1_ref, ...), custom_call_target="tpu_custom_call" | custom-call | flops 700000000 | bytes 4000000 | tf_op jit(solution)/shard_map/pallas_call | solution.py:199
  61.5 0.0 collective-permute-done.4.r1_ref
  61.5 0.0 collective-permute-done.6.r2_ref
  61.5 13.7 %collective-permute-done.8.r3_ref = bf16[2,240,512]{2,1,0:T(8,128)(2,1)S(1)} collective-permute-done((bf16[2,240,512]{2,1,0:T(8,128)(2,1)S(1)}, bf16[2,240,512]{2,1,0:T(8,128)(2,1)S(1)}, u32[]{:S(2)}, u32[]{:S(2)}) %collective-permute-start.8) | collective-permute-done | bytes 491552 | tf_op jit(solution)/shard_map/ppermute | solution.py:370
  75.2 3.3 %shard_map.73 = (bf16[2,3,256,512]{3,2,1,0:T(8,128)(2,1)}, f32[5,128,128]{2,1,0:T(8,128)S(1)}, f32[5,128,128]{2,1,0:T(8,128)S(1)}) custom-call(s32[2,2]{1,0:T(2,128)S(1)} %get-tuple-element.19.ids_ref, bf16[4,2,16,512]{3,2,1,0:T(8,128)(2,1)S(1)} %get-tuple-element.20.e0_ref, ...), custom_call_target="tpu_custom_call", output_to_operand_aliasing={{0}: (12, {})} | custom-call | flops 700000000 | bytes 4000000 | tf_op jit(solution)/shard_map/pallas_call | solution.py:199
  78.5 0.5 collective-permute-start.12
  79.0 1.3 collective-permute-done.12
  80.3 15.7 %all_to_all.10 = f32[16,40,128]{2,1,0:T(8,128)S(1)} all-to-all(f32[16,40,128]{2,1,0:T(8,128)S(1)} %bitcast.18), channel_id=1, replica_groups=mesh['y'=4,'z'=4,'core'=2,'x'=4] {'y','z'}, dimensions={0} | all-to-all | bytes 655360 | tf_op jit(solution)/shard_map/all_to_all | solution.py:342
  96.0 0.1 collective-permute-start.13
  96.1 2.6 %collective-permute-done.13 = f32[40,128]{1,0:T(8,128)S(1)} collective-permute-done((f32[40,128]{1,0:T(8,128)S(1)}, f32[40,128]{1,0:T(8,128)S(1)}, u32[]{:S(2)}, u32[]{:S(2)}) %collective-permute-start.13) | collective-permute-done | bytes 20512 | tf_op jit(solution)/shard_map/ppermute | solution.py:345
  98.7 0.6 collective-permute-start.14
  99.4 3.5 %collective-permute-done.14 = f32[40,128]{1,0:T(8,128)S(1)} collective-permute-done((f32[40,128]{1,0:T(8,128)S(1)}, f32[40,128]{1,0:T(8,128)S(1)}, u32[]{:S(2)}, u32[]{:S(2)}) %collective-permute-start.14) | collective-permute-done | bytes 20512 | tf_op jit(solution)/shard_map/ppermute | solution.py:345
  102.9 11.5 %all_to_all.11 = f32[16,40,128]{2,1,0:T(8,128)S(1)} all-to-all(f32[16,40,128]{2,1,0:T(8,128)S(1)} %broadcast_in_dim.3), channel_id=1, replica_groups=mesh['y'=4,'z'=4,'core'=2,'x'=4] {'y','z'}, dimensions={0} | all-to-all | bytes 655360 | tf_op jit(solution)/shard_map/all_to_all | solution.py:346
  114.4 5.2 %collective-permute-start.15 = (f32[5,128,128]{2,1,0:T(8,128)S(1)}, f32[5,128,128]{2,1,0:T(8,128)S(1)}, u32[]{:S(2)}, u32[]{:S(2)}) collective-permute-start(f32[5,128,128]{2,1,0:T(8,128)S(1)} %bitcast.8), channel_id=1, source_target_pairs={{0,4},{4,0},{1,5},{5,1},{2,6},{6,2},{3,7},{7,3},{8,12},{12,8},{9,1... | collective-permute-start | bytes 983048 | tf_op jit(solution)/shard_map/ppermute | solution.py:347
  119.7 1.3 collective-permute-done.15.other_ref
  120.9 16.0 %factor.1 = f32[512,512]{1,0:T(8,128)} custom-call(f32[5,128,128]{2,1,0:T(8,128)S(1)} %bitcast.9, f32[5,128,128]{2,1,0:T(8,128)S(1)} %collective-permute-done.15.other_ref), custom_call_target="tpu_custom_call" | custom-call | tf_op jit(solution)/shard_map/factor/pallas_call | solution.py:325
  (7 shorter events, 0.1 us)
Async XLA Ops:
  1.5 3.1 %collective-permute-start.3 = (s32[2,2]{1,0:T(2,128)S(1)}, s32[2,2]{1,0:T(2,128)S(1)}, u32[]{:S(2)}, u32[]{:S(2)}) collective-permute-start(s32[2,2]{1,0:T(2,128)S(1)} %get-tuple-element.19.ids_ref), channel_id=1, source_target_pairs={{0,1},{1,0},{2,3},{3,2},{4,5},{5,4},{6,7},{7,6},{8,9},{9,8},{10,11... | collective-permute-start | bytes 56 | tf_op jit(solution)/shard_map/ppermute | solution.py:363
  6.3 28.5 %collective-permute-start.9 = (bf16[2,240,512]{2,1,0:T(8,128)(2,1)S(1)}, bf16[2,240,512]{2,1,0:T(8,128)(2,1)S(1)}, u32[]{:S(2)}, u32[]{:S(2)}) collective-permute-start(bf16[2,240,512]{2,1,0:T(8,128)(2,1)S(1)} %get-tuple-element.28), channel_id=1, source_target_pairs={{0,1},{1,0},{2,3},{3,2},{4,5},{5,4},{6,7},{7,6},{8,9},{9,8},{10,11... | collective-permute-start | bytes 1474568 | tf_op jit(solution)/shard_map/ppermute | solution.py:370
  7.9 23.0 %collective-permute-start.2 = (bf16[4,2,16,512]{3,2,1,0:T(8,128)(2,1)S(1)}, bf16[4,2,16,512]{3,2,1,0:T(8,128)(2,1)S(1)}, u32[]{:S(2)}, u32[]{:S(2)}) collective-permute-start(bf16[4,2,16,512]{3,2,1,0:T(8,128)(2,1)S(1)} %get-tuple-element.20.e0_ref), channel_id=1, source_target_pairs={{0,3},{1,2},{2,1},{3,0},{4,7},{5,6},{6,5},{7,4},{8,11},{9,10},{10,... | collective-permute-start | bytes 393224 | tf_op jit(solution)/shard_map/ppermute | solution.py:365
  9.7 22.4 %collective-permute-start.1 = (bf16[4,2,16,512]{3,2,1,0:T(8,128)(2,1)S(1)}, bf16[4,2,16,512]{3,2,1,0:T(8,128)(2,1)S(1)}, u32[]{:S(2)}, u32[]{:S(2)}) collective-permute-start(bf16[4,2,16,512]{3,2,1,0:T(8,128)(2,1)S(1)} %get-tuple-element.20.e0_ref), channel_id=1, source_target_pairs={{0,2},{1,3},{2,0},{3,1},{4,6},{5,7},{6,4},{7,5},{8,10},{9,11},{10,... | collective-permute-start | bytes 393224 | tf_op jit(solution)/shard_map/ppermute | solution.py:365
  10.3 23.2 %collective-permute-start = (bf16[4,2,16,512]{3,2,1,0:T(8,128)(2,1)S(1)}, bf16[4,2,16,512]{3,2,1,0:T(8,128)(2,1)S(1)}, u32[]{:S(2)}, u32[]{:S(2)}) collective-permute-start(bf16[4,2,16,512]{3,2,1,0:T(8,128)(2,1)S(1)} %get-tuple-element.20.e0_ref), channel_id=1, source_target_pairs={{0,1},{1,0},{2,3},{3,2},{4,5},{5,4},{6,7},{7,6},{8,9},{9,8},{10,11... | collective-permute-start | bytes 393224 | tf_op jit(solution)/shard_map/ppermute | solution.py:365
  11.1 14.2 %collective-permute-start.5 = (s32[2,2]{1,0:T(2,128)S(1)}, s32[2,2]{1,0:T(2,128)S(1)}, u32[]{:S(2)}, u32[]{:S(2)}) collective-permute-start(s32[2,2]{1,0:T(2,128)S(1)} %get-tuple-element.19.ids_ref), channel_id=1, source_target_pairs={{0,2},{1,3},{2,0},{3,1},{4,6},{5,7},{6,4},{7,5},{8,10},{9,11},{10,... | collective-permute-start | bytes 56 | tf_op jit(solution)/shard_map/ppermute | solution.py:363
  25.3 3.6 %collective-permute-start.7 = (s32[2,2]{1,0:T(2,128)S(1)}, s32[2,2]{1,0:T(2,128)S(1)}, u32[]{:S(2)}, u32[]{:S(2)}) collective-permute-start(s32[2,2]{1,0:T(2,128)S(1)} %get-tuple-element.19.ids_ref), channel_id=1, source_target_pairs={{0,3},{1,2},{2,1},{3,0},{4,7},{5,6},{6,5},{7,4},{8,11},{9,10},{10,... | collective-permute-start | bytes 56 | tf_op jit(solution)/shard_map/ppermute | solution.py:363
  28.9 10.7 %collective-permute-start.10 = (bf16[2,240,512]{2,1,0:T(8,128)(2,1)S(1)}, bf16[2,240,512]{2,1,0:T(8,128)(2,1)S(1)}, u32[]{:S(2)}, u32[]{:S(2)}) collective-permute-start(bf16[2,240,512]{2,1,0:T(8,128)(2,1)S(1)} %get-tuple-element.29), channel_id=1, source_target_pairs={{0,2},{1,3},{2,0},{3,1},{4,6},{5,7},{6,4},{7,5},{8,10},{9,11},{10,... | collective-permute-start | bytes 1474568 | tf_op jit(solution)/shard_map/ppermute | solution.py:370
  30.8 6.9 %copy-start.2 = (f32[1,1,2,3,4,256]{5,4,3,2,1,0:T(4,128)S(1)}, f32[1,1,2,3,4,256]{5,4,3,2,1,0:T(4,128)}, u32[]{:S(2)}) copy-start(f32[1,1,2,3,4,256]{5,4,3,2,1,0:T(4,128)} %param.9) | copy-start | bytes 73732
  30.8 7.0 %copy-start = (s32[1,1,2,2,2,256]{5,4,3,2,1,0:T(2,128)S(1)}, s32[1,1,2,2,2,256]{5,4,3,2,1,0:T(2,128)}, u32[]{:S(2)}) copy-start(s32[1,1,2,2,2,256]{5,4,3,2,1,0:T(2,128)} %param.7) | copy-start | bytes 24580
  30.8 7.0 %copy-start.1 = (f32[1,1,2,2,2,256]{5,4,3,2,1,0:T(2,128)S(1)}, f32[1,1,2,2,2,256]{5,4,3,2,1,0:T(2,128)}, u32[]{:S(2)}) copy-start(f32[1,1,2,2,2,256]{5,4,3,2,1,0:T(2,128)} %param.8) | copy-start | bytes 24580
  30.8 27.5 %collective-permute-start.11 = (bf16[2,240,512]{2,1,0:T(8,128)(2,1)S(1)}, bf16[2,240,512]{2,1,0:T(8,128)(2,1)S(1)}, u32[]{:S(2)}, u32[]{:S(2)}) collective-permute-start(bf16[2,240,512]{2,1,0:T(8,128)(2,1)S(1)} %get-tuple-element.30), channel_id=1, source_target_pairs={{0,3},{1,2},{2,1},{3,0},{4,7},{5,6},{6,5},{7,4},{8,11},{9,10},{10,... | collective-permute-start | bytes 1474568 | tf_op jit(solution)/shard_map/ppermute | solution.py:370
  32.1 29.4 %collective-permute-start.4 = (bf16[2,240,512]{2,1,0:T(8,128)(2,1)S(1)}, bf16[2,240,512]{2,1,0:T(8,128)(2,1)S(1)}, u32[]{:S(2)}, u32[]{:S(2)}) collective-permute-start(bf16[2,240,512]{2,1,0:T(8,128)(2,1)S(1)} %get-tuple-element.22), channel_id=1, source_target_pairs={{0,1},{1,0},{2,3},{3,2},{4,5},{5,4},{6,7},{7,6},{8,9},{9,8},{10,11... | collective-permute-start | bytes 1474568 | tf_op jit(solution)/shard_map/ppermute | solution.py:370
  33.5 28.0 %collective-permute-start.6 = (bf16[2,240,512]{2,1,0:T(8,128)(2,1)S(1)}, bf16[2,240,512]{2,1,0:T(8,128)(2,1)S(1)}, u32[]{:S(2)}, u32[]{:S(2)}) collective-permute-start(bf16[2,240,512]{2,1,0:T(8,128)(2,1)S(1)} %get-tuple-element.23), channel_id=1, source_target_pairs={{0,2},{1,3},{2,0},{3,1},{4,6},{5,7},{6,4},{7,5},{8,10},{9,11},{10,... | collective-permute-start | bytes 1474568 | tf_op jit(solution)/shard_map/ppermute | solution.py:370
  34.8 40.4 %collective-permute-start.8 = (bf16[2,240,512]{2,1,0:T(8,128)(2,1)S(1)}, bf16[2,240,512]{2,1,0:T(8,128)(2,1)S(1)}, u32[]{:S(2)}, u32[]{:S(2)}) collective-permute-start(bf16[2,240,512]{2,1,0:T(8,128)(2,1)S(1)} %get-tuple-element.24), channel_id=1, source_target_pairs={{0,3},{1,2},{2,1},{3,0},{4,7},{5,6},{6,5},{7,4},{8,11},{9,10},{10,... | collective-permute-start | bytes 1474568 | tf_op jit(solution)/shard_map/ppermute | solution.py:370
  78.5 1.8 %collective-permute-start.12 = (f32[5,128,128]{2,1,0:T(8,128)S(1)}, f32[5,128,128]{2,1,0:T(8,128)S(1)}, u32[]{:S(2)}, u32[]{:S(2)}) collective-permute-start(f32[5,128,128]{2,1,0:T(8,128)S(1)} %get-tuple-element.35), channel_id=1, source_target_pairs={{0,4},{4,0},{1,5},{5,1},{2,6},{6,2},{3,7},{7,3},{8,12},{12,8},{9,1... | collective-permute-start | bytes 983048 | tf_op jit(solution)/shard_map/ppermute | solution.py:341
  96.0 2.7 %collective-permute-start.13 = (f32[40,128]{1,0:T(8,128)S(1)}, f32[40,128]{1,0:T(8,128)S(1)}, u32[]{:S(2)}, u32[]{:S(2)}) collective-permute-start(f32[40,128]{1,0:T(8,128)S(1)} %reduce_sum.9), channel_id=1, source_target_pairs={{0,1},{1,0},{2,3},{3,2},{4,5},{5,4},{6,7},{7,6},{8,9},{9,8},{10,11... | collective-permute-start | bytes 61448 | tf_op jit(solution)/shard_map/ppermute | solution.py:345
  98.7 4.1 %collective-permute-start.14 = (f32[40,128]{1,0:T(8,128)S(1)}, f32[40,128]{1,0:T(8,128)S(1)}, u32[]{:S(2)}, u32[]{:S(2)}) collective-permute-start(f32[40,128]{1,0:T(8,128)S(1)} %add.10), channel_id=1, source_target_pairs={{0,2},{1,3},{2,0},{3,1},{4,6},{5,7},{6,4},{7,5},{8,10},{9,11},{10,... | collective-permute-start | bytes 61448 | tf_op jit(solution)/shard_map/ppermute | solution.py:345
  114.4 6.5 %collective-permute-start.15 = (f32[5,128,128]{2,1,0:T(8,128)S(1)}, f32[5,128,128]{2,1,0:T(8,128)S(1)}, u32[]{:S(2)}, u32[]{:S(2)}) collective-permute-start(f32[5,128,128]{2,1,0:T(8,128)S(1)} %bitcast.8), channel_id=1, source_target_pairs={{0,4},{4,0},{1,5},{5,1},{2,6},{6,2},{3,7},{7,3},{8,12},{12,8},{9,1... | collective-permute-start | bytes 983048 | tf_op jit(solution)/shard_map/ppermute | solution.py:347
